TPU v7x, 32 devices: a whole 2x2x4 slice. The times are simulated.
32 devices in a mesh: sec: 4 (over y, x), wide: 8 (over z, core).
Axes of the slice: x: 2, y: 2, z: 4, core: 2. Of those that a mesh axis runs over, the one named last changes fastest.
Arguments:
- train_feats: bfloat16 [512, 512], P('wide'), may hold values from -0.26367188 to 0.26367188
- train_targets: float32 [512, 1000], P('wide'), may hold values from -6 to 6
- batch_idx: int32 [32], P('wide'), may hold values from 0 to 511, as said below
- centers: bfloat16 [65536, 512], P(('sec', 'wide')), may hold values from -0.26367188 to 0.26367188
- weights: bfloat16 [65536, 1000], P(('sec', 'wide')), may hold values from -0.0234375 to 0.0234375
- nys_idx: int32 [2048], P('wide'), may hold values from 0 to 65535, as said below
- eig_vecs: float32 [2048, 128], P('wide'), may hold values from -0.25 to 0.25
- eig_scale: float32 [128], replicated, may hold values from 0.2 to 1
Outputs:
- new_weights: bfloat16 [65536, 1000], P(('sec', 'wide'))
- residual: float32 [32, 1000], P('wide')
Inputs may be any that keep to these rules, and one draw needn't show every extreme that they name: `batch_idx`: entries k * 4 to (k + 1) * 4 - 1 name training rows k * 64 to (k + 1) * 64 - 1. For entry i, (nys_idx[i] // 2048) modulo (8) equals i // 256; the section, nys_idx[i] // 16384, is any; indices may repeat.
All inputs are finite; a program needn't handle non-finite values.
Results may differ from a plain program's by a relative error of at most 0.0054.
Values may be sent and summed in bfloat16 or wider, within the bound.
No kernel may reach another device: no remote copies, remote signals or barrier semaphores. Data moves between devices by JAX's collectives and lax.ppermute only.
A program may use at most 128 MiB of HBM per device.

v0:
```python
import math

import jax
import jax.numpy as jnp
from jax import lax
from jax.sharding import PartitionSpec as P


def shards(train_feats, train_targets, batch_idx, centers, weights, nys_idx, eig_vecs, eig_scale):
    pool_rows = train_feats.shape[0]
    batch_rows = batch_idx.shape[0]
    center_rows = centers.shape[0]
    feat_dim = centers.shape[1]
    classes = weights.shape[1]
    wide_count = lax.axis_size("wide")
    wide_pos = lax.axis_index("wide")
    sec_pos = lax.axis_index("sec")
    batch_total = batch_rows * wide_count
    local_rows = batch_idx - wide_pos * pool_rows
    my_feats = train_feats[local_rows]
    my_targets = train_targets[local_rows]
    cent_sq = jnp.sum(jnp.square(centers.astype(jnp.float32)), axis=1)
    length = 1.5 / math.sqrt(feat_dim)
    piece = lax.all_gather(my_feats, "wide", axis=0, tiled=True)
    cross = lax.dot_general(
        piece, centers, (((1,), (1,)), ((), ())), preferred_element_type=jnp.float32
    )
    row_sq = jnp.sum(jnp.square(piece.astype(jnp.float32)), axis=1)
    dist_sq = row_sq[:, None] + cent_sq[None, :] - 2.0 * cross
    kern = jnp.exp((1.4142 - jnp.sqrt(dist_sq)) / length).astype(jnp.bfloat16)
    rows = kern
    share = lax.psum_scatter(
        jnp.dot(rows, weights, preferred_element_type=jnp.float32),
        "wide",
        scatter_dimension=0,
        tiled=True,
    )
    pred = lax.psum(share, "sec")
    residual = pred - my_targets
    res_bf = residual.astype(jnp.bfloat16)
    rows = kern
    grad = lax.dot_general(
        rows,
        lax.all_gather(res_bf, "wide", axis=0, tiled=True),
        (((0,), (0,)), ((), ())),
        preferred_element_type=jnp.float32,
    )
    nys_local = nys_idx % center_rows
    nys_section = nys_idx // (center_rows * wide_count)
    owned = (nys_section == sec_pos).astype(jnp.float32)
    coords = grad[nys_local] * owned[:, None]
    proj = jnp.dot(eig_vecs.T, coords, precision=lax.Precision.HIGHEST)
    proj = lax.psum(proj, ("sec", "wide"))
    corr = jnp.dot(eig_vecs, eig_scale[:, None] * proj, precision=lax.Precision.HIGHEST)
    spread = jnp.zeros((center_rows, classes), jnp.float32).at[nys_local].add(corr * owned[:, None])
    update = 16.0 / batch_total * (grad - spread)
    new_weights = (weights.astype(jnp.float32) - update).astype(jnp.bfloat16)
    return (new_weights, residual)


def solution(mesh):
    return jax.shard_map(
        shards,
        mesh=mesh,
        in_specs=(
            P("wide", None),
            P("wide", None),
            P("wide"),
            P(("sec", "wide"), None),
            P(("sec", "wide"), None),
            P("wide"),
            P("wide", None),
            P(),
        ),
        out_specs=(P(("sec", "wide"), None), P("wide", None)),
        check_vma=False,
    )
```

profile of v0, /device:TPU:0, one launch (start us, length us, event | category | flops | bytes accessed | tf_op | source)
XLA Modules:
  0.0 304.2 jit_solution(17310374184672606950)
XLA Ops:
  7.2 0.0 copy-start
  7.2 0.0 copy-start.4
  7.2 0.0 copy-start.2
  7.2 0.0 all-reduce.6.cloned.1.call-start
  7.3 0.7 compare_select_fusion.1
  7.9 2.1 multiply_reduce_fusion
  10.0 1.4 gather_fusion
  11.4 15.8 %all-gather.1 = bf16[8,4,512]{2,1,0:T(4,128)(2,1)S(1)} all-gather(bf16[1,4,512]{2,1,0:T(4,128)(2,1)S(1)} %bitcast.16), channel_id=2, replica_groups=mesh['sec'=4,'wide'=8] {'wide'}, dimensions={0}, use_global_device_ids=true | all-gather | bytes 36864 | tf_op jit(solution)/shard_map/all_gather | solution.py:24
  27.2 0.1 multiply_reduce_fusion.1
  27.4 2.4 fusion.7
  29.7 4.1 %fusion.13 = f32[32,1000]{1,0:T(8,128)} fusion(bf16[32,2048]{1,0:T(8,128)(2,1)S(1)} %fusion.7, bf16[2048,1000]{0,1:T(8,128)(2,1)} %param.12), kind=kOutput, calls=%fused_computation.36 | convolution fusion | flops 131072000 | bytes 4355072 | tf_op jit(solution)/shard_map/dot_general | solution.py:33
  33.8 0.0 all-reduce.6.cloned.1.call-update
  33.8 0.0 all-reduce.4.cloned.1.call-start
  33.9 0.0 copy-done.2
  34.0 0.0 copy-done
  34.0 0.6 gather_fusion.1
  34.5 0.0 copy-done.4
  34.5 0.6 dynamic-slice
  35.8 54.2 %all-reduce.6.cloned.1.call-done = f32[32,1000]{1,0:T(8,128)} async-done(((f32[32,1000]{1,0:T(8,128)}), f32[32,1000]{1,0:T(8,128)}) %all-reduce.6.cloned.1.call-update) | async-done | bytes 128016
  90.0 0.8 constant_dynamic-slice_fusion
  90.7 16.0 %psum.14 = f32[4,1000]{1,0:T(4,128)S(1)} all-reduce(f32[4,1000]{1,0:T(4,128)S(1)} %constant_dynamic-slice_fusion), channel_id=1, replica_groups=mesh['sec'=4,'wide'=8] {'sec'}, use_global_device_ids=true, to_apply=%region_3.0 | all-reduce | flops 4000 | bytes 32000 | tf_op jit(solution)/shard_map/psum | solution.py:38
  106.7 0.6 convert_bitcast_fusion
  107.3 14.0 %all-gather.2 = bf16[8,4,1000]{2,1,0:T(4,128)(2,1)S(1)} all-gather(bf16[1,4,1000]{2,1,0:T(4,128)(2,1)S(1)} %get-tuple-element.2), channel_id=1, replica_groups=mesh['sec'=4,'wide'=8] {'wide'}, dimensions={0}, use_global_device_ids=true | all-gather | bytes 72000 | tf_op jit(solution)/shard_map/all_gather | solution.py:44
  121.3 4.4 %fusion.14 = f32[2048,1000]{0,1:T(8,128)} fusion(bf16[32,2048]{1,0:T(8,128)(2,1)S(1)} %fusion.7, bf16[32,1000]{1,0:T(8,128)(2,1)S(1)} %reshape.48), kind=kOutput, calls=%fused_computation.37 | convolution fusion | flops 131072000 | bytes 8387072 | tf_op jit(solution)/shard_map/dot_general | solution.py:42
  125.8 9.2 %copy.13 = f32[2048,1000]{1,0:T(8,128)} copy(f32[2048,1000]{0,1:T(8,128)} %fusion.14) | data formatting | bytes 16384000 | tf_op jit(solution)/shard_map/dot_general | solution.py:42
  135.0 0.0 copy-start.1
  135.0 0.0 copy-start.3
  135.0 5.0 %gather_fusion.2 = f32[256,1000]{1,0:T(8,128)S(1)} fusion(f32[2048,1000]{1,0:T(8,128)} %copy.13, s32[1024]{0:T(1024)S(1)} %pad_clamp_fusion), kind=kCustom, calls=%fused_computation.2 | custom fusion | bytes 2049024 | tf_op jit(solution)/shard_map/gather | solution.py:51
  140.0 0.0 copy-done.1
  140.0 1.6 convolution_bitcast_fusion
  141.6 0.0 all-reduce.4.cloned.1.call-update
  141.7 126.4 %all-reduce.4.cloned.1.call-done = f32[128,1000]{1,0:T(8,128)} async-done(((f32[128,1000]{1,0:T(8,128)}), f32[128,1000]{1,0:T(8,128)}) %all-reduce.4.cloned.1.call-update) | async-done | bytes 512016 | tf_op jit(solution)/shard_map/psum | solution.py:53
  268.1 0.0 copy-done.3
  268.1 2.1 fusion.8
  270.2 0.3 copy.14
  270.6 6.3 %scatter_custom_fusion = f32[2048,1000]{1,0:T(8,128)} fusion(s32[256]{0:T(256)S(1)} %compare_select_fusion, f32[256,1000]{1,0:T(8,128)S(1)} %copy.14, f32[]{:T(128)} %constant.45.clone.1), kind=kCustom, calls=%fused_computation.5 | custom fusion | flops 256000 | bytes 8192004 | tf_op jit(solution)/shard_map/scatter-add | solution.py:55
  276.9 9.2 %copy.15 = f32[2048,1000]{0,1:T(8,128)} copy(f32[2048,1000]{1,0:T(8,128)} %scatter_custom_fusion) | data formatting | bytes 16384000 | tf_op jit(solution)/shard_map/scatter-add | solution.py:55
  286.1 11.3 %subtract_convert_fusion = bf16[2048,1000]{0,1:T(8,128)(2,1)} fusion(f32[2048,1000]{0,1:T(8,128)} %fusion.14, f32[2048,1000]{0,1:T(8,128)} %copy.15, bf16[2048,1000]{0,1:T(8,128)(2,1)} %param.12), kind=kLoop, calls=%fused_computation.4 | loop fusion | flops 10240000 | bytes 24576000 | tf_op jit(solution)/shard_map/convert_element_type | solution.py:57
  (6 shorter events, 0.1 us)
Async XLA Ops:
  7.2 26.8 %copy-start = (f32[64,1000]{1,0:T(8,128)S(1)}, f32[64,1000]{1,0:T(8,128)}, u32[]{:S(2)}) copy-start(f32[64,1000]{1,0:T(8,128)} %param.9) | copy-start | bytes 768004
  7.2 27.4 %copy-start.4 = (u32[32]{0:T(128)S(1)}, u32[32]{0:T(128)}, u32[]{:S(2)}) copy-start(u32[32]{0:T(128)} %constant.59) | copy-start | bytes 388
  7.2 26.7 %copy-start.2 = (s32[256]{0:T(256)S(1)}, s32[256]{0:T(256)}, u32[]{:S(2)}) copy-start(s32[256]{0:T(256)} %param.13) | copy-start | bytes 3076
  7.2 82.8 %all-reduce.6.cloned.1.call-start = ((), (), s32[]{:S(2)}) async-start(), calls=%async_computation.1 | async-start | bytes 262144
  33.8 234.2 %all-reduce.4.cloned.1.call-start = ((), (), s32[]{:S(2)}) async-start(), calls=%async_computation | async-start | bytes 1048576 | tf_op jit(solution)/shard_map/psum | solution.py:53
  135.0 5.0 %copy-start.1 = (f32[256,128]{1,0:T(8,128)S(1)}, f32[256,128]{1,0:T(8,128)}, u32[]{:S(2)}) copy-start(f32[256,128]{1,0:T(8,128)} %param.14) | copy-start | bytes 393220
  135.0 133.1 %copy-start.3 = (f32[128]{0:T(128)S(1)}, f32[128]{0:T(128)}, u32[]{:S(2)}) copy-start(f32[128]{0:T(128)} %param.15) | copy-start | bytes 1540
Sparse Core Ops, SparseCore 0:
  34.0 55.9 all-reduce.5
  141.8 126.2 all-reduce.3
where the time goes:
time: 305 us; the launch traced here: 304 us
  waiting for transfers between devices  181 us (59%)
  blocking collectives  45.7 us (15%)
  local copies, waits for them, and re-layouts  27.2 us (9%)
  other arithmetic  21.1 us (7%)
  between operations  14.8 us (5%)
  matrix products  14.7 us (5%)
    psum x1, waiting for transfers between devices, shards(): proj = lax.psum(proj, ('sec', 'wide'))  126 us
    unnamed x3, waiting for transfers between devices  54.2 us
    psum x1, blocking collectives, shards(): pred = lax.psum(share, 'sec')  16 us
    all_gather x1, blocking collectives, shards(): piece = lax.all_gather(my_feats, 'wide', axis=0, tiled=True)  15.8 us
    all_gather x1, blocking collectives, shards(): lax.all_gather(res_bf, 'wide', axis=0, tiled=True)  14 us
    convert_element_type x1, other arithmetic, shards(): new_weights = (weights.astype(jnp.float32) - update).astype(jnp.bfloat16)  11.3 us
    dot_general x1, local copies, waits for them, and re-layouts, shards(): lax.dot_general(rows, lax.all_gather(res_bf, 'wide', axis=0, tiled=True),...  9.24 us
    scatter-add x1, local copies, waits for them, and re-layouts, shards(): jnp.zeros((center_rows, classes), jnp.float32).at[nys_local]  9.23 us
  transfers between devices with their start and end apart: 2, of which 2 were waited for; matrix products, arithmetic and copies ran while one was open for 0% of the time, Pallas kernels for 0%

commit v1 on v0

v1 whole, which is shorter than its diff:
```python
import math

import jax
import jax.numpy as jnp
from jax import lax
from jax.sharding import PartitionSpec as P

HIGH = lax.Precision.HIGHEST


def spread_out(rows, axes):
    count = lax.axis_size(axes)
    return lax.all_to_all(jnp.broadcast_to(rows[None], (count,) + rows.shape), axes, 0, 0, tiled=False)


def shards(train_feats, train_targets, batch_idx, centers, weights, nys_idx, eig_vecs, eig_scale):
    pool_rows = train_feats.shape[0]
    batch_rows = batch_idx.shape[0]
    center_rows = centers.shape[0]
    feat_dim = centers.shape[1]
    classes = weights.shape[1]
    wide_count = lax.axis_size("wide")
    sec_count = lax.axis_size("sec")
    wide_pos = lax.axis_index("wide")
    sec_pos = lax.axis_index("sec")
    batch_total = batch_rows * wide_count
    share_rows = batch_rows // sec_count
    local_rows = batch_idx - wide_pos * pool_rows
    picked = (local_rows[:, None] == jnp.arange(pool_rows)[None, :]).astype(jnp.bfloat16)
    my_feats = jnp.dot(picked, train_feats, preferred_element_type=jnp.float32).astype(jnp.bfloat16)
    piece = spread_out(my_feats, "wide")
    piece = jnp.transpose(piece, (1, 0, 2)).reshape(batch_total, feat_dim)
    my_targets = lax.dynamic_slice_in_dim(train_targets[local_rows], sec_pos * share_rows, share_rows, 0)

    nys_local = nys_idx % center_rows
    owned = nys_idx // (center_rows * wide_count) == sec_pos
    place = jnp.where(owned, nys_local, center_rows)
    hot = (place[None, :] == jnp.arange(center_rows)[:, None]).astype(jnp.float32)
    vecs = jnp.dot(hot, eig_vecs, precision=HIGH)

    cent_sq = jnp.sum(jnp.square(centers.astype(jnp.float32)), axis=1)
    length = 1.5 / math.sqrt(feat_dim)
    cross = lax.dot_general(
        piece, centers, (((1,), (1,)), ((), ())), preferred_element_type=jnp.float32
    )
    row_sq = jnp.sum(jnp.square(piece.astype(jnp.float32)), axis=1)
    dist_sq = row_sq[:, None] + cent_sq[None, :] - 2.0 * cross
    kern = jnp.exp((1.4142 - jnp.sqrt(dist_sq)) / length).astype(jnp.bfloat16)

    part = jnp.concatenate(
        [
            jnp.dot(kern, weights, preferred_element_type=jnp.float32),
            jnp.dot(kern.astype(jnp.float32), vecs, precision=HIGH),
        ],
        axis=1,
    )
    part = part.reshape(sec_count, share_rows, wide_count, -1).transpose(0, 2, 1, 3)
    part = part.reshape(sec_count * wide_count, share_rows, -1)
    mine = jnp.sum(lax.all_to_all(part, ("sec", "wide"), 0, 0, tiled=False), axis=0)
    mine = jnp.concatenate([mine[:, :classes] - my_targets, mine[:, classes:]], axis=1)
    both = spread_out(mine, ("sec", "wide")).reshape(sec_count, wide_count, share_rows, -1)
    both = both.transpose(0, 2, 1, 3).reshape(batch_rows, wide_count, -1)
    residual = lax.dynamic_index_in_dim(both[:, :, :classes], wide_pos, 1, keepdims=False)
    both = both.reshape(batch_total, -1)
    res_bf = both[:, :classes].astype(jnp.bfloat16)
    coords = both[:, classes:]

    drop = lax.dot_general(coords * eig_scale[None, :], vecs, (((1,), (1,)), ((), ())), precision=HIGH)
    drop_hi = drop.astype(jnp.bfloat16)
    drop_lo = (drop - drop_hi.astype(jnp.float32)).astype(jnp.bfloat16)
    factors = jnp.concatenate([kern, -drop_hi, -drop_lo], axis=0)
    grad = lax.dot_general(
        factors,
        jnp.concatenate([res_bf, res_bf, res_bf], axis=0),
        (((0,), (0,)), ((), ())),
        preferred_element_type=jnp.float32,
    )
    new_weights = (weights.astype(jnp.float32) - 16.0 / batch_total * grad).astype(jnp.bfloat16)
    return (new_weights, residual)


def solution(mesh):
    return jax.shard_map(
        shards,
        mesh=mesh,
        in_specs=(
            P("wide", None),
            P("wide", None),
            P("wide"),
            P(("sec", "wide"), None),
            P(("sec", "wide"), None),
            P("wide"),
            P("wide", None),
            P(),
        ),
        out_specs=(P(("sec", "wide"), None), P("wide", None)),
        check_vma=False,
    )
```

time: 305 us -> 55.7 us (0.18)
  waiting for transfers between devices: 181 us -> 17.2 us
  blocking collectives: 45.7 us -> 0 us
  local copies, waits for them, and re-layouts: 27.2 us -> 3.59 us
  other arithmetic: 21.1 us -> 3.84 us
  between operations: 14.8 us -> 0.76 us
  starting transfers between devices: 0.08 us -> 14 us
    psum x1 -> x0, waiting for transfers between devices: 126 us -> none  [shards(): proj = lax.psum(proj, ('sec', 'wide'))]
    unnamed x3 -> x0, waiting for transfers between devices: 54.2 us -> none
    all_gather x2 -> x0, blocking collectives: 29.8 us -> none  [the longest x1 15.8 us: shards(): piece = lax.all_gather(my_feats, 'wide', axis=0, tiled=True)]
    all_to_all x0 -> x3, waiting for transfers between devices: none -> 17.2 us  [the longest x2 9.41 us: spread_out(): lax.all_to_all(jnp.broadcast_to(rows[None], (count,) + rows.shape), axes,...]
    psum x1 -> x0, blocking collectives: 16 us -> none  [shards(): pred = lax.psum(share, 'sec')]
    all_to_all x0 -> x3, starting transfers between devices: none -> 14 us  [the longest x2 8.93 us: spread_out(): lax.all_to_all(jnp.broadcast_to(rows[None], (count,) + rows.shape), axes,...]
    convert_element_type x2 -> x0, other arithmetic: 11.3 us -> none  [the longest x1 11.3 us: shards(): new_weights = (weights.astype(jnp.float32) - update).astype(jnp.bfloat16)]
    dot_general x1 -> x0, local copies, waits for them, and re-layouts: 9.24 us -> none  [shards(): lax.dot_general(rows, lax.all_gather(res_bf, 'wide', axis=0, tiled=True),...]
  transfers between devices with their start and end apart: 2 -> 3, of which waited for: 2 -> 3; matrix products, arithmetic and copies ran while one was open for 0% -> 10% of each run, Pallas kernels for 0% -> 0%
where the time goes in v1:
time: 55.7 us; the launch traced here: 55.2 us
  waiting for transfers between devices  17.2 us (31%)
  matrix products  15.8 us (28%)
  starting transfers between devices  14 us (25%)
  other arithmetic  3.84 us (7%)
  local copies, waits for them, and re-layouts  3.59 us (6%)
  between operations  0.76 us (1%)
    all_to_all x2, waiting for transfers between devices, spread_out(): lax.all_to_all(jnp.broadcast_to(rows[None], (count,) + rows.shape), axes,...  9.41 us
    all_to_all x2, starting transfers between devices, spread_out(): lax.all_to_all(jnp.broadcast_to(rows[None], (count,) + rows.shape), axes,...  8.93 us
    all_to_all x1, waiting for transfers between devices, shards(): lax.all_to_all(part, ('sec', 'wide'), 0, 0, tiled=False)  7.77 us
    dot_general x1, matrix products, shards(): lax.dot_general(factors, jnp.concatenate([res_bf, res_bf, res_bf], axis=0...  5.41 us
    all_to_all x1, starting transfers between devices, shards(): lax.all_to_all(part, ('sec', 'wide'), 0, 0, tiled=False)  5.04 us
    dot_general x1, matrix products, shards(): jnp.dot(kern, weights, preferred_element_type=jnp.float32)  3.41 us
    dot_general x1, matrix products, shards(): lax.dot_general(piece, centers, (((1,), (1,)), ((), ())), preferred_eleme...  2.35 us
    reduce_sum x1, other arithmetic, shards(): cent_sq = jnp.sum(jnp.square(centers.astype(jnp.float32)), axis=1)  2.07 us
  transfers between devices with their start and end apart: 3, of which 3 were waited for; matrix products, arithmetic and copies ran while one was open for 10% of the time, Pallas kernels for 0%

profile of v1, /device:TPU:0, one launch (start us, length us, event | category | flops | bytes accessed | tf_op | source)
XLA Modules:
  0.0 55.2 jit_solution(5743985897512429036)
XLA Ops:
  0.6 0.0 copy-start
  0.7 0.7 %compare_select_fusion = (s32[4]{0:T(128)S(1)}, s32[4]{0:T(128)S(1)}) fusion(s32[4]{0:T(128)} %param.10, s32[]{:T(128)S(6)} %mul.23), kind=kLoop, calls=%fused_computation.41 | loop fusion | flops 16 | bytes 52 | tf_op jit(solution)/shard_map/select_n | solution.py:33
  1.4 1.0 %convolution_convert_fusion = bf16[4,512]{1,0:T(4,128)(2,1)S(1)} fusion(bf16[64,512]{1,0:T(8,128)(2,1)} %param.8, s32[4]{0:T(128)S(1)} %get-tuple-element.3), kind=kOutput, calls=%fused_computation.12 | convolution fusion | flops 264448 | bytes 69648 | tf_op jit(solution)/shard_map/dot_general | solution.py:30
  2.4 0.6 %broadcast_in_dim.10 = bf16[8,4,512]{2,1,0:T(4,128)(2,1)} broadcast(bf16[4,512]{1,0:T(4,128)(2,1)S(1)} %convolution_convert_fusion), dimensions={1,2} | broadcast | bytes 36864 | tf_op jit(solution)/shard_map/broadcast_in_dim | solution.py:13
  3.0 6.4 %all-to-all-start = ((bf16[8,4,512]{2,1,0:T(4,128)(2,1)}), bf16[8,4,512]{2,1,0:T(4,128)(2,1)S(1)}, u32[]{:S(2)}, u32[]{:S(2)}) async-start(bf16[8,4,512]{2,1,0:T(4,128)(2,1)} %broadcast_in_dim.10), calls=%async_computation | async-start | bytes 65536 | tf_op jit(solution)/shard_map/all_to_all | solution.py:13
  9.4 0.7 %compare_select_fusion.1 = s32[256]{0:T(256)S(1)} fusion(s32[256]{0:T(256)} %param.13, s32[]{:T(128)S(6)} %axis_index.25), kind=kLoop, calls=%fused_computation.44 | loop fusion | flops 6400 | bytes 2052 | tf_op jit(solution)/shard_map/jit(_where)/select_n | solution.py:37
  10.0 1.9 %fusion.6 = f32[2048,128]{1,0:T(8,128)S(1)} fusion(f32[256,128]{1,0:T(8,128)} %param.14, s32[256]{0:T(256)S(1)} %compare_select_fusion.1), kind=kOutput, calls=%fused_computation.11 | convolution fusion | flops 805830656 | bytes 1180672 | tf_op jit(solution)/shard_map/dot_general | solution.py:39
  12.0 2.1 %multiply_reduce_fusion = f32[2048]{0:T(1024)S(1)} fusion(bf16[2048,512]{1,0:T(8,128)(2,1)} %param.11), kind=kLoop, calls=%fused_computation.2 | loop fusion | flops 3143680 | bytes 2105344 | tf_op jit(solution)/shard_map/reduce_sum | solution.py:41
  14.1 1.1 %all-to-all-done = bf16[8,4,512]{2,1,0:T(4,128)(2,1)S(1)} async-done(((bf16[8,4,512]{2,1,0:T(4,128)(2,1)}), bf16[8,4,512]{2,1,0:T(4,128)(2,1)S(1)}, u32[]{:S(2)}, u32[]{:S(2)}) %all-to-all-start) | async-done | bytes 32800 | tf_op jit(solution)/shard_map/all_to_all | solution.py:13
  15.1 0.1 multiply_reduce_fusion.1
  15.2 0.1 add.32
  15.3 2.3 %fusion.5 = bf16[32,2048]{1,0:T(8,128)(2,1)S(1)} fusion(bf16[2048,512]{1,0:T(8,128)(2,1)} %param.11, f32[2048]{0:T(1024)S(1)} %multiply_reduce_fusion, f32[32]{0:T(128)S(1)} %add.32, bf16[8,4,512]{2,1,0:T(4,128)(2,1)S(1)} %all-to-all-done), kind=kOutput, calls=%fused_computation.9 | convolution fusion | flops 67502080 | bytes 2269312 | tf_op jit(solution)/shard_map/dot_general | solution.py:43
  17.6 0.0 copy-start.1
  17.7 3.4 %fusion.25 = f32[32,1000]{1,0:T(8,128)S(1)} fusion(bf16[32,2048]{1,0:T(8,128)(2,1)S(1)} %fusion.5, bf16[2048,1000]{0,1:T(8,128)(2,1)} %param.12), kind=kOutput, calls=%fused_computation.54 | convolution fusion | flops 131072000 | bytes 4355072 | tf_op jit(solution)/shard_map/dot_general | solution.py:52
  21.1 0.5 fusion.26
  21.6 0.1 maximum_bitcast_fusion
  21.7 0.8 %copy.11 = f32[32,1,1128]{2,1,0:T(1,128)} copy(f32[32,1,1128]{2,0,1:T(8,128)S(1)} %maximum_bitcast_fusion) | data formatting | bytes 288768 | tf_op jit(solution)/shard_map/reshape;transpose;reshape | solution.py:58
  22.5 5.0 %all-to-all-start.1 = ((f32[32,1,1128]{2,1,0:T(1,128)}), f32[32,1,1128]{2,1,0:T(1,128)S(1)}, u32[]{:S(2)}, u32[]{:S(2)}) async-start(f32[32,1,1128]{2,1,0:T(1,128)} %copy.11), calls=%async_computation.1 | async-start | bytes 294912 | tf_op jit(solution)/shard_map/all_to_all | solution.py:59
  27.5 0.0 copy-done
  27.5 0.6 %gather_fusion = f32[4,1000]{1,0:T(4,128)S(1)} fusion(f32[64,1000]{1,0:T(8,128)S(1)} %copy-done, s32[1024]{0:T(1024)S(1)} %pad_clamp_fusion), kind=kCustom, calls=%fused_computation | custom fusion | bytes 32016 | tf_op jit(solution)/shard_map/gather | solution.py:33
  28.1 7.8 %all-to-all-done.1 = f32[32,1,1128]{2,1,0:T(1,128)S(1)} async-done(((f32[32,1,1128]{2,1,0:T(1,128)}), f32[32,1,1128]{2,1,0:T(1,128)S(1)}, u32[]{:S(2)}, u32[]{:S(2)}) %all-to-all-start.1) | async-done | bytes 144416 | tf_op jit(solution)/shard_map/all_to_all | solution.py:59
  35.9 0.1 reduce_sum.31
  36.0 0.1 slice.24
  36.1 0.1 maximum_reduce_fusion
  36.2 0.7 %broadcast_in_dim.13 = f32[32,1,1128]{2,1,0:T(1,128)} broadcast(f32[1128]{0:T(1024)S(1)} %maximum_reduce_fusion), dimensions={2} | broadcast | bytes 148896 | tf_op jit(solution)/shard_map/broadcast_in_dim | solution.py:13
  36.9 2.6 %all-to-all-start.2 = ((f32[32,1,1128]{2,1,0:T(1,128)}), f32[32,1,1128]{2,1,0:T(1,128)S(1)}, u32[]{:S(2)}, u32[]{:S(2)}) async-start(f32[32,1,1128]{2,1,0:T(1,128)} %broadcast_in_dim.13), calls=%async_computation.2 | async-start | bytes 294912 | tf_op jit(solution)/shard_map/all_to_all | solution.py:13
  39.5 8.4 %all-to-all-done.2 = f32[32,1,1128]{2,1,0:T(1,128)S(1)} async-done(((f32[32,1,1128]{2,1,0:T(1,128)}), f32[32,1,1128]{2,1,0:T(1,128)S(1)}, u32[]{:S(2)}, u32[]{:S(2)}) %all-to-all-start.2) | async-done | bytes 144416 | tf_op jit(solution)/shard_map/all_to_all | solution.py:13
  47.9 0.0 copy-done.1
  47.9 1.2 %convert_negate_fusion = (bf16[32,2048]{1,0:T(8,128)(2,1)S(1)}, bf16[32,2048]{1,0:T(8,128)(2,1)S(1)}) fusion(f32[2048,128]{1,0:T(8,128)S(1)} %fusion.6, f32[32,1128]{1,0:T(8,128)S(1)} %bitcast.25, f32[128]{0:T(128)S(1)} %copy-done.1), kind=kOutput, calls=%fused_computation.30 | convolution fusion | flops 101060608 | bytes 1327616 | tf_op jit(solution)/shard_map/dot_general | solution.py:68
  49.2 0.6 %copy.24 = f32[4,1,1000]{2,0,1:T(4,128)} copy(f32[4,1,1000]{2,1,0:T(1,128)S(1)} %constant_dynamic-slice_fusion) | data formatting | bytes 32000
  49.8 5.4 %subtract_convert_fusion = bf16[2048,1000]{0,1:T(8,128)(2,1)} fusion(bf16[2048,1000]{0,1:T(8,128)(2,1)} %param.12, bf16[32,2048]{1,0:T(8,128)(2,1)S(1)} %get-tuple-element.5, bf16[32,2048]{1,0:T(8,128)(2,1)S(1)} %get-tuple-element.4, bf16[32,2048]{1,0:T(8,128)(2,1)S(1)} %fusion.5, bf16[32,1000]{1,0:T(8,128)(2,1)S(1)} %slice.32), kind=kOutput, calls=%fused_computation.1 | convolution fusion | flops 403163648 | bytes 8649216 | tf_op jit(solution)/shard_map/dot_general | solution.py:72
  (7 shorter events, 0.1 us)
Async XLA Ops:
  0.6 26.9 %copy-start = (f32[64,1000]{1,0:T(8,128)S(1)}, f32[64,1000]{1,0:T(8,128)}, u32[]{:S(2)}) copy-start(f32[64,1000]{1,0:T(8,128)} %param.9) | copy-start | bytes 768004
  3.0 12.1 %all-to-all-start = ((bf16[8,4,512]{2,1,0:T(4,128)(2,1)}), bf16[8,4,512]{2,1,0:T(4,128)(2,1)S(1)}, u32[]{:S(2)}, u32[]{:S(2)}) async-start(bf16[8,4,512]{2,1,0:T(4,128)(2,1)} %broadcast_in_dim.10), calls=%async_computation | async-start | bytes 65536 | tf_op jit(solution)/shard_map/all_to_all | solution.py:13
  17.6 30.2 %copy-start.1 = (f32[128]{0:T(128)S(1)}, f32[128]{0:T(128)}, u32[]{:S(2)}) copy-start(f32[128]{0:T(128)} %param.15) | copy-start | bytes 1540
  22.5 13.4 %all-to-all-start.1 = ((f32[32,1,1128]{2,1,0:T(1,128)}), f32[32,1,1128]{2,1,0:T(1,128)S(1)}, u32[]{:S(2)}, u32[]{:S(2)}) async-start(f32[32,1,1128]{2,1,0:T(1,128)} %copy.11), calls=%async_computation.1 | async-start | bytes 294912 | tf_op jit(solution)/shard_map/all_to_all | solution.py:59
  36.9 10.9 %all-to-all-start.2 = ((f32[32,1,1128]{2,1,0:T(1,128)}), f32[32,1,1128]{2,1,0:T(1,128)S(1)}, u32[]{:S(2)}, u32[]{:S(2)}) async-start(f32[32,1,1128]{2,1,0:T(1,128)} %broadcast_in_dim.13), calls=%async_computation.2 | async-start | bytes 294912 | tf_op jit(solution)/shard_map/all_to_all | solution.py:13

commit v2 on v1

v2 whole, which is shorter than its diff:
```python
import functools
import math

import jax
import jax.numpy as jnp
from jax import lax
from jax.experimental import pallas as pl
from jax.experimental.pallas import tpu as pltpu
from jax.sharding import PartitionSpec as P

VMEM_GRANT = 24 << 20
HIGH = lax.Precision.HIGHEST
NT = (((1,), (1,)), ((), ()))
NN = (((1,), (0,)), ((), ()))


def dot32(a, b, dims):
    return lax.dot_general(a, b, dims, preferred_element_type=jnp.float32)


def halves(x):
    top = x.astype(jnp.bfloat16)
    return top, (x - top.astype(jnp.float32)).astype(jnp.bfloat16)


def share_body(feats_ref, cents_ref, cent_sq_ref, wt_ref, vecs_ref, kern_ref, part_ref, *, step):
    center_rows, feat_dim = cents_ref.shape
    classes = wt_ref.shape[0]
    length = 1.5 / math.sqrt(feat_dim)
    feats = feats_ref[...]
    wide_feats = feats.astype(jnp.float32)
    row_sq = jnp.sum(wide_feats * wide_feats, axis=1, keepdims=True)
    for start in range(0, center_rows, step):
        cols = pl.ds(start, step)
        cross = dot32(feats, cents_ref[cols, :], NT)
        dist_sq = jnp.maximum(row_sq + cent_sq_ref[:, cols] - 2.0 * cross, 0.0)
        kern_ref[:, cols] = jnp.exp((1.4142 - jnp.sqrt(dist_sq)) / length).astype(jnp.bfloat16)
    kern = kern_ref[...]
    vec_hi, vec_lo = halves(vecs_ref[...])
    part_ref[:, 0, :classes] = dot32(kern, wt_ref[...], NT)
    part_ref[:, 0, classes:] = dot32(kern, vec_hi, NN) + dot32(kern, vec_lo, NN)


def update_body(pos_ref, both_ref, scale_ref, kern_ref, vecs_ref, wt_ref, out_ref, res_ref, left_ref, *, rate, sections):
    classes = wt_ref.shape[0]
    batch_total = both_ref.shape[0]
    wide_count = batch_total // sections

    @pl.when(pl.program_id(0) == 0)
    def _():
        turned = both_ref[:, 0, :classes].T.astype(jnp.bfloat16)
        left_ref[...] = jnp.concatenate([turned, turned, turned], axis=1)
        for s in range(sections):
            res_ref[s, :] = both_ref[s * wide_count + pos_ref[0], 0, :classes]

    coords_hi, coords_lo = halves(both_ref[:, 0, classes:] * scale_ref[...])
    vec_hi, vec_lo = halves(vecs_ref[...])
    drop = dot32(coords_hi, vec_hi, NT) + dot32(coords_hi, vec_lo, NT) + dot32(coords_lo, vec_hi, NT)
    drop_hi, drop_lo = halves(-drop)
    grad = dot32(left_ref[...], jnp.concatenate([kern_ref[...], drop_hi, drop_lo], axis=0), NN)
    out_ref[...] = (wt_ref[...].astype(jnp.float32) - rate * grad).astype(jnp.bfloat16)


def shards(train_feats, train_targets, batch_idx, centers, weights, nys_idx, eig_vecs, eig_scale):
    pool_rows = train_feats.shape[0]
    batch_rows = batch_idx.shape[0]
    center_rows, feat_dim = centers.shape
    classes = weights.shape[1]
    eig_count = eig_vecs.shape[1]
    wide_count = lax.axis_size("wide")
    sec_count = lax.axis_size("sec")
    wide_pos = lax.axis_index("wide")
    sec_pos = lax.axis_index("sec")
    batch_total = batch_rows * wide_count
    cols = classes + eig_count
    assert batch_rows == sec_count
    vmem = pl.BlockSpec(memory_space=pltpu.VMEM)

    local_rows = batch_idx - wide_pos * pool_rows
    picked = (local_rows[None, :, None] == jnp.arange(pool_rows)[None, None, :]).astype(jnp.bfloat16)
    picked = jnp.broadcast_to(picked, (wide_count, batch_rows, pool_rows))
    copies = lax.dot_general(picked, train_feats, (((2,), (0,)), ((), ())), preferred_element_type=jnp.float32)
    piece = lax.all_to_all(copies.astype(jnp.bfloat16), "wide", 0, 0, tiled=False)
    piece = jnp.transpose(piece, (1, 0, 2)).reshape(batch_total, feat_dim)
    my_target = lax.dynamic_slice_in_dim(train_targets[local_rows], sec_pos, 1, 0)

    owned = nys_idx // (center_rows * wide_count) == sec_pos
    place = jnp.where(owned, nys_idx % center_rows, center_rows)
    hot = (place[None, :] == jnp.arange(center_rows)[:, None]).astype(jnp.float32)
    vecs = jnp.dot(hot, eig_vecs, precision=HIGH)
    cent_sq = jnp.sum(jnp.square(centers.astype(jnp.float32)), axis=1)[None, :]

    turned_weights = weights.T
    kern, part = pl.pallas_call(
        functools.partial(share_body, step=min(512, center_rows)),
        out_shape=(
            jax.ShapeDtypeStruct((batch_total, center_rows), jnp.bfloat16),
            jax.ShapeDtypeStruct((batch_total, 1, cols), jnp.float32),
        ),
        in_specs=[vmem] * 5,
        out_specs=(vmem, vmem),
        compiler_params=pltpu.CompilerParams(vmem_limit_bytes=VMEM_GRANT),
        name="share",
    )(piece, centers, cent_sq, turned_weights, vecs)

    mine = jnp.sum(lax.all_to_all(part, ("sec", "wide"), 0, 0, tiled=False), axis=0)
    mine = jnp.concatenate([mine[:, :classes] - my_target, mine[:, classes:]], axis=1)
    both = lax.all_to_all(
        jnp.broadcast_to(mine[None], (batch_total, 1, cols)), ("sec", "wide"), 0, 0, tiled=False
    )

    block = min(256, center_rows)
    new_turned, residual = pl.pallas_call(
        functools.partial(update_body, rate=16.0 / batch_total, sections=sec_count),
        grid=(center_rows // block,),
        out_shape=(
            jax.ShapeDtypeStruct((classes, center_rows), jnp.bfloat16),
            jax.ShapeDtypeStruct((batch_rows, classes), jnp.float32),
        ),
        in_specs=[
            pl.BlockSpec(memory_space=pltpu.SMEM),
            pl.BlockSpec((batch_total, 1, cols), lambda i: (0, 0, 0)),
            pl.BlockSpec((1, eig_count), lambda i: (0, 0)),
            pl.BlockSpec((batch_total, block), lambda i: (0, i)),
            pl.BlockSpec((block, eig_count), lambda i: (i, 0)),
            pl.BlockSpec((classes, block), lambda i: (0, i)),
        ],
        out_specs=(
            pl.BlockSpec((classes, block), lambda i: (0, i)),
            pl.BlockSpec((batch_rows, classes), lambda i: (0, 0)),
        ),
        scratch_shapes=[pltpu.VMEM((classes, 3 * batch_total), jnp.bfloat16)],
        compiler_params=pltpu.CompilerParams(vmem_limit_bytes=VMEM_GRANT),
        name="update",
    )(wide_pos[None], both, eig_scale[None, :], kern, vecs, turned_weights)
    return (new_turned.T, residual)


def solution(mesh):
    return jax.shard_map(
        shards,
        mesh=mesh,
        in_specs=(
            P("wide", None),
            P("wide", None),
            P("wide"),
            P(("sec", "wide"), None),
            P(("sec", "wide"), None),
            P("wide"),
            P("wide", None),
            P(),
        ),
        out_specs=(P(("sec", "wide"), None), P("wide", None)),
        check_vma=False,
    )
```

time: 55.7 us -> 53.6 us (0.962)
  matrix products: 15.8 us -> 2.89 us
  blocking collectives: 0 us -> 10.2 us
  Pallas kernels: 0 us -> 9.66 us
  waiting for transfers between devices: 17.2 us -> 8.81 us
  starting transfers between devices: 14 us -> 11.4 us
  local copies, waits for them, and re-layouts: 3.59 us -> 5.71 us
    dot_general x6 -> x1, matrix products: 13.9 us -> 0.96 us  [shards(): lax.dot_general(picked, train_feats, (((2,), (0,)), ((), ())), preferred_...]
    all_to_all x0 -> x1, blocking collectives: none -> 10.2 us  [shards(): lax.all_to_all(jnp.broadcast_to(mine[None], (batch_total, 1, cols)), ('se...]
    pallas_call x0 -> x2, Pallas kernels: none -> 9.66 us  [the longest x1 6.85 us: shards(): pl.pallas_call(functools.partial(update_body, rate=16.0 / batch_total, se...]
    all_to_all x2 -> x1, waiting for transfers between devices: 9.41 us -> 1.04 us  [shards(): lax.all_to_all(copies.astype(jnp.bfloat16), 'wide', 0, 0, tiled=False)]
    unnamed x6 -> x10, local copies, waits for them, and re-layouts: 0.64 us -> 4.34 us
    all_to_all x2 -> x1, starting transfers between devices: 8.93 us -> 6.35 us  [shards(): lax.all_to_all(copies.astype(jnp.bfloat16), 'wide', 0, 0, tiled=False)]
    broadcast_in_dim x2 -> x1, local copies, waits for them, and re-layouts: 1.37 us -> 0.08 us  [shards(): jnp.broadcast_to(mine[None], (batch_total, 1, cols))]
    another operation x1 -> x0, local copies, waits for them, and re-layouts: 0.82 us -> none  [shards(): part = part.reshape(sec_count * wide_count, share_rows, -1)]
  transfers between devices with their start and end apart: 3 -> 2, of which waited for: 3 -> 2; matrix products, arithmetic and copies ran while one was open for 10% -> 10% of each run, Pallas kernels for 0% -> 0%
where the time goes in v2:
time: 53.6 us; the launch traced here: 53.2 us
  starting transfers between devices  11.4 us (21%)
  blocking collectives  10.2 us (19%)
  Pallas kernels  9.66 us (18%)
  waiting for transfers between devices  8.81 us (16%)
  local copies, waits for them, and re-layouts  5.71 us (11%)
  other arithmetic  3.85 us (7%)
  matrix products  2.89 us (5%)
  between operations  0.73 us (1%)
    all_to_all x1, blocking collectives, shards(): lax.all_to_all(jnp.broadcast_to(mine[None], (batch_total, 1, cols)), ('se...  10.2 us
    all_to_all x1, waiting for transfers between devices, shards(): lax.all_to_all(part, ('sec', 'wide'), 0, 0, tiled=False)  7.77 us
    pallas_call x1, Pallas kernels, shards(): pl.pallas_call(functools.partial(update_body, rate=16.0 / batch_total, se...  6.85 us
    all_to_all x1, starting transfers between devices, shards(): lax.all_to_all(copies.astype(jnp.bfloat16), 'wide', 0, 0, tiled=False)  6.35 us
    all_to_all x1, starting transfers between devices, shards(): lax.all_to_all(part, ('sec', 'wide'), 0, 0, tiled=False)  5.04 us
    unnamed x10, local copies, waits for them, and re-layouts  4.34 us
    pallas_call x1, Pallas kernels, shards(): pl.pallas_call(functools.partial(share_body, step=min(512, center_rows)),...  2.81 us
    reduce_sum x1, other arithmetic, shards(): cent_sq = jnp.sum(jnp.square(centers.astype(jnp.float32)), axis=1)[None, :]  2.07 us
  transfers between devices with their start and end apart: 2, of which 2 were waited for; matrix products, arithmetic and copies ran while one was open for 10% of the time, Pallas kernels for 0%

profile of v2, /device:TPU:0, one launch (start us, length us, event | category | flops | bytes accessed | tf_op | source)
XLA Modules:
  0.0 53.2 jit_solution(6217708162087949993)
XLA Ops:
  0.6 0.0 copy-start
  0.6 0.0 copy-start.3
  0.7 0.8 %compare_select_fusion = (s32[4]{0:T(128)S(1)}, s32[4]{0:T(128)S(1)}) fusion(s32[4]{0:T(128)} %param.10, s32[]{:T(128)S(6)} %mul.3), kind=kLoop, calls=%fused_computation.12 | loop fusion | flops 16 | bytes 52 | tf_op jit(solution)/shard_map/select_n | solution.py:85
  1.5 0.1 fusion.4
  1.5 1.0 %convolution_convert_fusion = bf16[8,4,512]{2,0,1:T(8,128)(2,1)S(1)} fusion(bf16[64,512]{1,0:T(8,128)(2,1)} %param.8, bf16[4,64]{1,0:T(4,128)(2,1)S(1)} %fusion.4), kind=kOutput, calls=%fused_computation.4 | convolution fusion | flops 2113536 | bytes 98816 | tf_op jit(solution)/shard_map/dot_general | solution.py:82
  2.5 0.6 %copy.10 = bf16[8,4,512]{2,1,0:T(4,128)(2,1)} copy(bf16[8,4,512]{2,0,1:T(8,128)(2,1)S(1)} %convolution_convert_fusion) | data formatting | bytes 65536 | tf_op jit(solution)/shard_map/convert_element_type | solution.py:83
  3.2 6.4 %all-to-all-start = ((bf16[8,4,512]{2,1,0:T(4,128)(2,1)}), bf16[8,4,512]{2,1,0:T(4,128)(2,1)S(1)}, u32[]{:S(2)}, u32[]{:S(2)}) async-start(bf16[8,4,512]{2,1,0:T(4,128)(2,1)} %copy.10), calls=%async_computation | async-start | bytes 65536 | tf_op jit(solution)/shard_map/all_to_all | solution.py:83
  9.5 0.7 %compare_select_fusion.1 = s32[256]{0:T(256)S(1)} fusion(s32[256]{0:T(256)} %param.13, s32[]{:T(128)S(6)} %axis_index.25), kind=kLoop, calls=%fused_computation.16 | loop fusion | flops 6400 | bytes 2052 | tf_op jit(solution)/shard_map/jit(_where)/select_n | solution.py:88
  10.2 1.9 %fusion.vecs_ref = f32[2048,128]{1,0:T(8,128)S(1)} fusion(f32[256,128]{1,0:T(8,128)} %param.14, s32[256]{0:T(256)S(1)} %compare_select_fusion.1), kind=kOutput, calls=%fused_computation.3 | convolution fusion | flops 805830656 | bytes 1180672 | tf_op jit(solution)/shard_map/dot_general | solution.py:90
  12.1 2.1 %multiply_reduce_fusion = f32[2048]{0:T(1024)S(1)} fusion(bf16[2048,512]{1,0:T(8,128)(2,1)} %cents_ref.1), kind=kLoop, calls=%fused_computation.1 | loop fusion | flops 3143680 | bytes 2105344 | tf_op jit(solution)/shard_map/reduce_sum | solution.py:91
  14.2 1.0 %all-to-all-done = bf16[8,4,512]{2,1,0:T(4,128)(2,1)S(1)} async-done(((bf16[8,4,512]{2,1,0:T(4,128)(2,1)}), bf16[8,4,512]{2,1,0:T(4,128)(2,1)S(1)}, u32[]{:S(2)}, u32[]{:S(2)}) %all-to-all-start) | async-done | bytes 32800 | tf_op jit(solution)/shard_map/all_to_all | solution.py:83
  15.3 0.0 copy-done.3
  15.3 0.0 copy-start.1
  15.3 2.2 %copy-done.1 = bf16[2048,1000]{0,1:T(8,128)(2,1)S(1)} copy-done((bf16[2048,1000]{0,1:T(8,128)(2,1)S(1)}, bf16[2048,1000]{0,1:T(8,128)(2,1)}, u32[]{:S(2)}) %copy-start.1) | copy-done | bytes 4096024
  17.4 0.0 copy-start.4
  17.4 2.8 %share.1 = (bf16[32,2048]{1,0:T(8,128)(2,1)S(1)}, f32[32,1,1128]{2,1,0:T(1,128)}) custom-call(bf16[32,512]{1,0:T(8,128)(2,1)S(1)} %bitcast.15, bf16[2048,512]{1,0:T(8,128)(2,1)S(1)} %copy-done.3, f32[1,2048]{1,0:T(1,128)S(1)} %bitcast.16, bf16[1000,2048]{1,0:T(8,128)(2,1)S(1)} %bitcast.13, f32[2048,128]{1,0:T(8,128)S(1)} %fusion.vecs_ref), custom_call_target="tpu_custom_call" | custom-call | tf_op jit(solution)/shard_map/share/pallas_call | solution.py:94
  20.2 5.0 %all-to-all-start.1 = ((f32[32,1,1128]{2,1,0:T(1,128)}), f32[32,1,1128]{2,1,0:T(1,128)S(1)}, u32[]{:S(2)}, u32[]{:S(2)}) async-start(f32[32,1,1128]{2,1,0:T(1,128)} %get-tuple-element.6), calls=%async_computation.1 | async-start | bytes 294912 | tf_op jit(solution)/shard_map/all_to_all | solution.py:106
  25.3 0.0 copy-done
  25.3 0.6 %gather_fusion = f32[4,1000]{1,0:T(4,128)S(1)} fusion(f32[64,1000]{1,0:T(8,128)S(1)} %copy-done, s32[1024]{0:T(1024)S(1)} %pad_clamp_fusion), kind=kCustom, calls=%fused_computation | custom fusion | bytes 32016 | tf_op jit(solution)/shard_map/gather | solution.py:85
  25.9 7.8 %all-to-all-done.1 = f32[32,1,1128]{2,1,0:T(1,128)S(1)} async-done(((f32[32,1,1128]{2,1,0:T(1,128)}), f32[32,1,1128]{2,1,0:T(1,128)S(1)}, u32[]{:S(2)}, u32[]{:S(2)}) %all-to-all-start.1) | async-done | bytes 144416 | tf_op jit(solution)/shard_map/all_to_all | solution.py:106
  33.7 0.1 reduce_sum.21
  33.8 0.1 slice.11
  33.9 0.1 maximum_reduce_fusion
  33.9 0.1 broadcast_in_dim.36
  34.0 10.2 %all_to_all.15.both_ref = f32[32,1,1128]{2,1,0:T(1,128)S(1)} all-to-all(f32[32,1,1128]{2,1,0:T(1,128)S(1)} %broadcast_in_dim.36), channel_id=1, replica_groups=mesh['sec'=4,'wide'=8] {'sec','wide'}, dimensions={0} | all-to-all | bytes 288768 | tf_op jit(solution)/shard_map/all_to_all | solution.py:108
  44.2 0.0 copy-done.4
  44.2 0.0 copy-start.2
  44.2 2.2 %copy-done.2 = bf16[2048,1000]{0,1:T(8,128)(2,1)S(1)} copy-done((bf16[2048,1000]{0,1:T(8,128)(2,1)S(1)}, bf16[2048,1000]{0,1:T(8,128)(2,1)}, u32[]{:S(2)}) %copy-start.2) | copy-done | bytes 4096024
  46.4 6.8 %update.1 = (bf16[1000,2048]{1,0:T(8,128)(2,1)}, f32[4,1000]{1,0:T(4,128)}) custom-call(s32[1]{0:T(128)} %bitcast.pos_ref, f32[32,1,1128]{2,1,0:T(1,128)S(1)} %all_to_all.15.both_ref, f32[1,128]{1,0:T(1,128)S(1)} %bitcast.17, bf16[32,2048]{1,0:T(8,128)(2,1)S(1)} %get-tuple-element.7.kern_ref, f32[2048,128]{1,0:T(8,128)S(1)} %fusion.vecs_ref, ...), custom_call_target="tpu_custom_call" | custom-call | tf_op jit(solution)/shard_map/update/pallas_call | solution.py:113
  (4 shorter events, 0.0 us)
Async XLA Ops:
  0.6 24.7 %copy-start = (f32[64,1000]{1,0:T(8,128)S(1)}, f32[64,1000]{1,0:T(8,128)}, u32[]{:S(2)}) copy-start(f32[64,1000]{1,0:T(8,128)} %param.9) | copy-start | bytes 768004
  0.6 14.6 %copy-start.3 = (bf16[2048,512]{1,0:T(8,128)(2,1)S(1)}, bf16[2048,512]{1,0:T(8,128)(2,1)}, u32[]{:S(2)}) copy-start(bf16[2048,512]{1,0:T(8,128)(2,1)} %cents_ref.1) | copy-start | bytes 6291460
  3.2 12.1 %all-to-all-start = ((bf16[8,4,512]{2,1,0:T(4,128)(2,1)}), bf16[8,4,512]{2,1,0:T(4,128)(2,1)S(1)}, u32[]{:S(2)}, u32[]{:S(2)}) async-start(bf16[8,4,512]{2,1,0:T(4,128)(2,1)} %copy.10), calls=%async_computation | async-start | bytes 65536 | tf_op jit(solution)/shard_map/all_to_all | solution.py:83
  15.3 2.2 %copy-start.1 = (bf16[2048,1000]{0,1:T(8,128)(2,1)S(1)}, bf16[2048,1000]{0,1:T(8,128)(2,1)}, u32[]{:S(2)}) copy-start(bf16[2048,1000]{0,1:T(8,128)(2,1)} %param.12) | copy-start | bytes 12288004
  17.4 26.8 %copy-start.4 = (f32[128]{0:T(128)S(1)}, f32[128]{0:T(128)}, u32[]{:S(2)}) copy-start(f32[128]{0:T(128)} %param.15) | copy-start | bytes 1540
  20.2 13.4 %all-to-all-start.1 = ((f32[32,1,1128]{2,1,0:T(1,128)}), f32[32,1,1128]{2,1,0:T(1,128)S(1)}, u32[]{:S(2)}, u32[]{:S(2)}) async-start(f32[32,1,1128]{2,1,0:T(1,128)} %get-tuple-element.6), calls=%async_computation.1 | async-start | bytes 294912 | tf_op jit(solution)/shard_map/all_to_all | solution.py:106
  44.2 2.2 %copy-start.2 = (bf16[2048,1000]{0,1:T(8,128)(2,1)S(1)}, bf16[2048,1000]{0,1:T(8,128)(2,1)}, u32[]{:S(2)}) copy-start(bf16[2048,1000]{0,1:T(8,128)(2,1)} %param.12) | copy-start | bytes 12288004

commit v3 on v2

v3 whole, which is shorter than its diff:
```python
import functools
import math

import jax
import jax.numpy as jnp
from jax import lax
from jax.experimental import pallas as pl
from jax.experimental.pallas import tpu as pltpu
from jax.sharding import PartitionSpec as P

VMEM_GRANT = 16 << 20
NT = (((1,), (1,)), ((), ()))
NN = (((1,), (0,)), ((), ()))


def dot32(a, b, dims):
    return lax.dot_general(a, b, dims, preferred_element_type=jnp.float32)


def halves(x):
    top = x.astype(jnp.bfloat16)
    return top, (x - top.astype(jnp.float32)).astype(jnp.bfloat16)


def in_hbm(x):
    return pltpu.with_memory_space_constraint(x, pltpu.HBM)


def gather_body(pos_ref, idx_hbm, rows_hbm, out_ref, idx_ref, rows_ref, sems):
    get_idx = pltpu.make_async_copy(idx_hbm, idx_ref, sems.at[0])
    get_rows = pltpu.make_async_copy(rows_hbm, rows_ref, sems.at[1])
    get_idx.start()
    get_rows.start()
    get_idx.wait()
    pool_rows = rows_ref.shape[0]
    copies, batch_rows = out_ref.shape[:2]
    shape = (batch_rows, pool_rows)
    row = lax.broadcasted_iota(jnp.int32, shape, 0)
    wanted = jnp.zeros(shape, jnp.int32)
    for j in range(batch_rows):
        wanted = jnp.where(row == j, idx_ref[j] - pos_ref[0] * pool_rows, wanted)
    picked = (lax.broadcasted_iota(jnp.int32, shape, 1) == wanted).astype(jnp.bfloat16)
    get_rows.wait()
    rows = dot32(picked, rows_ref[...], NN).astype(jnp.bfloat16)
    for w in range(copies):
        out_ref[w] = rows


def stage_body(
    pos_ref, nys_hbm, eig_hbm, cents_hbm, cents_ref, cent_sq_ref, vecs_ref, nys_ref, eig_ref, sems, *, step
):
    pairs = ((nys_hbm, nys_ref), (eig_hbm, eig_ref), (cents_hbm, cents_ref))
    gets = [pltpu.make_async_copy(src, dst, sems.at[i]) for i, (src, dst) in enumerate(pairs)]
    for get in gets:
        get.start()
    gets[0].wait()
    gets[1].wait()
    center_rows = cents_ref.shape[0]
    nys_count = nys_ref.shape[1]
    eig_hi, eig_lo = halves(eig_ref[...])
    place = nys_ref[...] - pos_ref[0] * center_rows
    for start in range(0, center_rows, step):
        at = lax.broadcasted_iota(jnp.int32, (step, nys_count), 0) + start
        hot = (at == place).astype(jnp.bfloat16)
        vecs_ref[pl.ds(start, step), :] = dot32(hot, eig_hi, NN) + dot32(hot, eig_lo, NN)
    gets[2].wait()
    ones = jnp.ones((8, cents_ref.shape[1]), jnp.bfloat16)
    for start in range(0, center_rows, step):
        rows = cents_ref[pl.ds(start, step), :].astype(jnp.float32)
        top, low = halves(rows * rows)
        total = dot32(ones, top, NT) + dot32(ones, low, NT)
        cent_sq_ref[:, pl.ds(start, step)] = total[:1]


def fetch(src_hbm, dst_ref, sems, step):
    gets = []
    for i in range(src_hbm.shape[1] // step):
        cols = pl.ds(i * step, step)
        gets.append(pltpu.make_async_copy(src_hbm.at[:, cols], dst_ref.at[:, cols], sems.at[i]))
        gets[-1].start()
    return gets


def share_body(feats_ref, cents_ref, cent_sq_ref, vecs_ref, wt_hbm, kern_ref, part_ref, wt_ref, sems, *, step):
    gets = fetch(wt_hbm, wt_ref, sems, step)
    center_rows, feat_dim = cents_ref.shape
    classes = wt_ref.shape[0]
    length = 1.5 / math.sqrt(feat_dim)
    feats = feats_ref[...]
    wide_feats = feats.astype(jnp.float32)
    row_sq = jnp.sum(wide_feats * wide_feats, axis=1, keepdims=True)
    for start in range(0, center_rows, step):
        cols = pl.ds(start, step)
        cross = dot32(feats, cents_ref[cols, :], NT)
        dist_sq = jnp.maximum(row_sq + cent_sq_ref[:, cols] - 2.0 * cross, 0.0)
        kern_ref[:, cols] = jnp.exp((1.4142 - jnp.sqrt(dist_sq)) / length).astype(jnp.bfloat16)
    vec_hi, vec_lo = halves(vecs_ref[...])
    part_ref[:, 0, classes:] = dot32(kern_ref[...], vec_hi, NN) + dot32(kern_ref[...], vec_lo, NN)
    total = None
    for i, get in enumerate(gets):
        cols = pl.ds(i * step, step)
        get.wait()
        term = dot32(kern_ref[:, cols], wt_ref[:, cols], NT)
        total = term if total is None else total + term
    part_ref[:, 0, :classes] = total


def update_body(
    pos_ref, both_ref, scale_ref, kern_ref, vecs_ref, wt_hbm, out_hbm, res_ref,
    left_ref, wt_ref, new_ref, get_sems, put_sems, *, rate, sections, step
):
    gets = fetch(wt_hbm, wt_ref, get_sems, step)
    classes = wt_ref.shape[0]
    wide_count = both_ref.shape[0] // sections
    turned = both_ref[:, 0, :classes].T.astype(jnp.bfloat16)
    left_ref[...] = jnp.concatenate([turned, turned, turned], axis=1)
    coords_hi, coords_lo = halves(both_ref[:, 0, classes:] * scale_ref[...])
    puts = []
    for i, get in enumerate(gets):
        cols = pl.ds(i * step, step)
        vec_hi, vec_lo = halves(vecs_ref[cols, :])
        drop = dot32(coords_hi, vec_hi, NT) + dot32(coords_hi, vec_lo, NT) + dot32(coords_lo, vec_hi, NT)
        drop_hi, drop_lo = halves(-drop)
        grad = dot32(left_ref[...], jnp.concatenate([kern_ref[:, cols], drop_hi, drop_lo], axis=0), NN)
        get.wait()
        new_ref[:, cols] = (wt_ref[:, cols].astype(jnp.float32) - rate * grad).astype(jnp.bfloat16)
        puts.append(pltpu.make_async_copy(new_ref.at[:, cols], out_hbm.at[:, cols], put_sems.at[i]))
        puts[-1].start()
    for s in range(sections):
        res_ref[s, :] = both_ref[s * wide_count + pos_ref[0], 0, :classes]
    for put in puts:
        put.wait()


def shards(train_feats, train_targets, batch_idx, centers, weights, nys_idx, eig_vecs, eig_scale):
    pool_rows = train_feats.shape[0]
    batch_rows = batch_idx.shape[0]
    center_rows, feat_dim = centers.shape
    classes = weights.shape[1]
    eig_count = eig_vecs.shape[1]
    wide_count = lax.axis_size("wide")
    sec_count = lax.axis_size("sec")
    wide_pos = lax.axis_index("wide")
    sec_pos = lax.axis_index("sec")
    batch_total = batch_rows * wide_count
    cols = classes + eig_count
    assert batch_rows == sec_count
    vmem = pl.BlockSpec(memory_space=pltpu.VMEM)
    smem = pl.BlockSpec(memory_space=pltpu.SMEM)
    hbm = pl.BlockSpec(memory_space=pltpu.HBM)

    params = pltpu.CompilerParams(vmem_limit_bytes=VMEM_GRANT)
    step = min(512, center_rows)

    copies = pl.pallas_call(
        gather_body,
        out_shape=jax.ShapeDtypeStruct((wide_count, batch_rows, feat_dim), jnp.bfloat16),
        in_specs=[smem, hbm, hbm],
        out_specs=vmem,
        scratch_shapes=[
            pltpu.SMEM((batch_rows,), jnp.int32),
            pltpu.VMEM(train_feats.shape, train_feats.dtype),
            pltpu.SemaphoreType.DMA((2,)),
        ],
        compiler_params=params,
        name="gather",
    )(wide_pos[None], in_hbm(batch_idx), in_hbm(train_feats))
    piece = lax.all_to_all(copies, "wide", 0, 0, tiled=False)
    piece = jnp.transpose(piece, (1, 0, 2)).reshape(batch_total, feat_dim)
    my_target = lax.dynamic_slice_in_dim(train_targets[batch_idx - wide_pos * pool_rows], sec_pos, 1, 0)

    turned_weights = in_hbm(weights.T)
    staged_centers, cent_sq, vecs = pl.pallas_call(
        functools.partial(stage_body, step=step),
        out_shape=(
            jax.ShapeDtypeStruct(centers.shape, centers.dtype),
            jax.ShapeDtypeStruct((1, center_rows), jnp.float32),
            jax.ShapeDtypeStruct((center_rows, eig_count), jnp.float32),
        ),
        in_specs=[smem, hbm, hbm, hbm],
        out_specs=(vmem, vmem, vmem),
        scratch_shapes=[
            pltpu.VMEM((1, nys_idx.shape[0]), jnp.int32),
            pltpu.VMEM(eig_vecs.shape, jnp.float32),
            pltpu.SemaphoreType.DMA((3,)),
        ],
        compiler_params=params,
        cost_estimate=pl.CostEstimate(flops=1 << 31, bytes_accessed=16 << 20, transcendentals=0),
        name="stage",
    )(
        (sec_pos * wide_count + wide_pos)[None],
        in_hbm(nys_idx[None, :]),
        in_hbm(eig_vecs),
        in_hbm(centers),
    )

    slabs = center_rows // step
    kern, part = pl.pallas_call(
        functools.partial(share_body, step=step),
        out_shape=(
            jax.ShapeDtypeStruct((batch_total, center_rows), jnp.bfloat16),
            jax.ShapeDtypeStruct((batch_total, 1, cols), jnp.float32),
        ),
        in_specs=[vmem] * 4 + [hbm],
        out_specs=(vmem, vmem),
        scratch_shapes=[pltpu.VMEM((classes, center_rows), jnp.bfloat16), pltpu.SemaphoreType.DMA((slabs,))],
        compiler_params=params,
        name="share",
    )(piece, staged_centers, cent_sq, vecs, turned_weights)

    mine = jnp.sum(lax.all_to_all(part, ("sec", "wide"), 0, 0, tiled=False), axis=0)
    mine = jnp.concatenate([mine[:, :classes] - my_target, mine[:, classes:]], axis=1)
    both = lax.all_to_all(
        jnp.broadcast_to(mine[None], (batch_total, 1, cols)), ("sec", "wide"), 0, 0, tiled=False
    )

    new_turned, residual = pl.pallas_call(
        functools.partial(update_body, rate=16.0 / batch_total, sections=sec_count, step=step),
        out_shape=(
            jax.ShapeDtypeStruct((classes, center_rows), jnp.bfloat16),
            jax.ShapeDtypeStruct((batch_rows, classes), jnp.float32),
        ),
        in_specs=[smem] + [vmem] * 4 + [hbm],
        out_specs=(hbm, vmem),
        scratch_shapes=[
            pltpu.VMEM((classes, 3 * batch_total), jnp.bfloat16),
            pltpu.VMEM((classes, center_rows), jnp.bfloat16),
            pltpu.VMEM((classes, center_rows), jnp.bfloat16),
            pltpu.SemaphoreType.DMA((slabs,)),
            pltpu.SemaphoreType.DMA((slabs,)),
        ],
        compiler_params=params,
        name="update",
    )(wide_pos[None], both, eig_scale[None, :], kern, vecs, turned_weights)
    return (new_turned.T, residual)


def solution(mesh):
    return jax.shard_map(
        shards,
        mesh=mesh,
        in_specs=(
            P("wide", None),
            P("wide", None),
            P("wide"),
            P(("sec", "wide"), None),
            P(("sec", "wide"), None),
            P("wide"),
            P("wide", None),
            P(),
        ),
        out_specs=(P(("sec", "wide"), None), P("wide", None)),
        check_vma=False,
    )
```

time: 53.6 us -> 47.6 us (0.89)
  Pallas kernels: 9.66 us -> 15.2 us
  local copies, waits for them, and re-layouts: 5.71 us -> 0.75 us
  other arithmetic: 3.85 us -> 0.21 us
  matrix products: 2.89 us -> 0 us
  starting transfers between devices: 11.4 us -> 9.7 us
  waiting for transfers between devices: 8.81 us -> 10.5 us
    pallas_call x1 -> x3, Pallas kernels: 2.81 us -> 8.31 us  [the longest x1 3.71 us: shards(): pl.pallas_call(functools.partial(share_body, step=step), out_shape=(jax.S...]
    unnamed x10 -> x6, local copies, waits for them, and re-layouts: 4.34 us -> 0.02 us
    dot_general x2 -> x0, matrix products: 2.89 us -> none  [the longest x1 1.93 us: shards(): vecs = jnp.dot(hot, eig_vecs, precision=HIGH)]
    reduce_sum x1 -> x0, other arithmetic: 2.07 us -> none  [shards(): cent_sq = jnp.sum(jnp.square(centers.astype(jnp.float32)), axis=1)[None, :]]
    all_to_all x1, waiting for transfers between devices: 1.04 us -> 2.76 us  [shards(): piece = lax.all_to_all(copies, 'wide', 0, 0, tiled=False)]
    all_to_all x1, starting transfers between devices: 5.04 us -> 3.33 us  [shards(): lax.all_to_all(part, ('sec', 'wide'), 0, 0, tiled=False)]
    select_n x2 -> x1, other arithmetic: 1.5 us -> 0.01 us  [shards(): train_targets[batch_idx - wide_pos * pool_rows]]
    convert_element_type x1 -> x0, local copies, waits for them, and re-layouts: 0.64 us -> none  [shards(): copies.astype(jnp.bfloat16)]
  transfers between devices with their start and end apart: 2 -> 2, of which waited for: 2 -> 2; matrix products, arithmetic and copies ran while one was open for 10% -> 1% of each run, Pallas kernels for 0% -> 6%
where the time goes in v3:
time: 47.6 us; the launch traced here: 47.2 us
  Pallas kernels  15.2 us (32%)
  waiting for transfers between devices  10.5 us (22%)
  blocking collectives  10.2 us (21%)
  starting transfers between devices  9.7 us (20%)
  local copies, waits for them, and re-layouts  0.75 us (2%)
  between operations  0.75 us (2%)
    all_to_all x1, blocking collectives, shards(): lax.all_to_all(jnp.broadcast_to(mine[None], (batch_total, 1, cols)), ('se...  10.2 us
    all_to_all x1, waiting for transfers between devices, shards(): lax.all_to_all(part, ('sec', 'wide'), 0, 0, tiled=False)  7.74 us
    pallas_call x1, Pallas kernels, shards(): pl.pallas_call(functools.partial(update_body, rate=16.0 / batch_total, se...  6.85 us
    all_to_all x1, starting transfers between devices, shards(): piece = lax.all_to_all(copies, 'wide', 0, 0, tiled=False)  6.37 us
    pallas_call x1, Pallas kernels, shards(): pl.pallas_call(functools.partial(share_body, step=step), out_shape=(jax.S...  3.71 us
    all_to_all x1, starting transfers between devices, shards(): lax.all_to_all(part, ('sec', 'wide'), 0, 0, tiled=False)  3.33 us
    pallas_call x1, Pallas kernels, shards(): pl.pallas_call(functools.partial(stage_body, step=step), out_shape=(jax.S...  2.96 us
    all_to_all x1, waiting for transfers between devices, shards(): piece = lax.all_to_all(copies, 'wide', 0, 0, tiled=False)  2.76 us
  transfers between devices with their start and end apart: 2, of which 2 were waited for; matrix products, arithmetic and copies ran while one was open for 1% of the time, Pallas kernels for 6%

profile of v3, /device:TPU:0, one launch (start us, length us, event | category | flops | bytes accessed | tf_op | source)
XLA Modules:
  0.0 47.2 jit_solution(16709274944415642089)
XLA Ops:
  0.6 0.0 copy-start
  0.6 1.6 %gather.7 = bf16[8,4,512]{2,1,0:T(4,128)(2,1)} custom-call(s32[1]{0:T(128)} %bitcast.pos_ref, s32[4]{0:T(128)} %idx_hbm.1, bf16[64,512]{1,0:T(8,128)(2,1)} %rows_hbm.1), custom_call_target="tpu_custom_call" | custom-call | tf_op jit(solution)/shard_map/gather/pallas_call | solution.py:155
  2.3 6.4 %all-to-all-start = ((bf16[8,4,512]{2,1,0:T(4,128)(2,1)}), bf16[8,4,512]{2,1,0:T(4,128)(2,1)S(1)}, u32[]{:S(2)}, u32[]{:S(2)}) async-start(bf16[8,4,512]{2,1,0:T(4,128)(2,1)} %gather.7), calls=%async_computation | async-start | bytes 65536 | tf_op jit(solution)/shard_map/all_to_all | solution.py:168
  8.7 3.0 %stage.1 = (bf16[2048,512]{1,0:T(8,128)(2,1)S(1)}, f32[1,2048]{1,0:T(1,128)S(1)}, f32[2048,128]{1,0:T(8,128)S(1)}) custom-call(s32[1]{0:T(128)} %bitcast.3.pos_ref, s32[1,256]{1,0:T(1,128)} %bitcast.16, f32[256,128]{1,0:T(8,128)} %eig_hbm.1, bf16[2048,512]{1,0:T(8,128)(2,1)} %cents_hbm.1), custom_call_target="tpu_custom_call" | custom-call | flops 2147483648 | bytes 16777216 | tf_op jit(solution)/shard_map/stage/pallas_call | solution.py:173
  11.6 0.0 copy-start.2
  11.6 2.8 %all-to-all-done = bf16[8,4,512]{2,1,0:T(4,128)(2,1)S(1)} async-done(((bf16[8,4,512]{2,1,0:T(4,128)(2,1)}), bf16[8,4,512]{2,1,0:T(4,128)(2,1)S(1)}, u32[]{:S(2)}, u32[]{:S(2)}) %all-to-all-start) | async-done | bytes 32800 | tf_op jit(solution)/shard_map/all_to_all | solution.py:168
  14.4 0.0 copy-start.1
  14.4 3.7 %share.1 = (bf16[32,2048]{1,0:T(8,128)(2,1)S(1)}, f32[32,1,1128]{2,1,0:T(1,128)}) custom-call(bf16[32,512]{1,0:T(8,128)(2,1)S(1)} %bitcast.10, bf16[2048,512]{1,0:T(8,128)(2,1)S(1)} %get-tuple-element.9.cents_ref, f32[1,2048]{1,0:T(1,128)S(1)} %get-tuple-element.10.cent_sq_ref, f32[2048,128]{1,0:T(8,128)S(1)} %get-tuple-element.11.vecs_ref, ...), custom_call_target="tpu_custom_call" | custom-call | tf_op jit(solution)/shard_map/share/pallas_call | solution.py:198
  18.1 3.3 %all-to-all-start.1 = ((f32[32,1,1128]{2,1,0:T(1,128)}), f32[32,1,1128]{2,1,0:T(1,128)S(1)}, u32[]{:S(2)}, u32[]{:S(2)}) async-start(f32[32,1,1128]{2,1,0:T(1,128)} %get-tuple-element.12), calls=%async_computation.1 | async-start | bytes 294912 | tf_op jit(solution)/shard_map/all_to_all | solution.py:211
  21.5 0.0 copy-done.2
  21.5 0.0 copy-done
  21.5 0.6 %gather_fusion = f32[4,1000]{1,0:T(4,128)S(1)} fusion(f32[64,1000]{1,0:T(8,128)S(1)} %copy-done, s32[1024]{0:T(1024)S(1)} %pad_clamp_fusion), kind=kCustom, calls=%fused_computation | custom fusion | bytes 32016 | tf_op jit(solution)/shard_map/gather | solution.py:170
  22.1 7.7 %all-to-all-done.1 = f32[32,1,1128]{2,1,0:T(1,128)S(1)} async-done(((f32[32,1,1128]{2,1,0:T(1,128)}), f32[32,1,1128]{2,1,0:T(1,128)S(1)}, u32[]{:S(2)}, u32[]{:S(2)}) %all-to-all-start.1) | async-done | bytes 144416 | tf_op jit(solution)/shard_map/all_to_all | solution.py:211
  29.8 0.1 reduce_sum.11
  30.0 0.1 slice.11
  30.0 0.1 maximum_reduce_fusion
  30.1 0.1 broadcast_in_dim.29
  30.2 10.2 %all_to_all.15.both_ref = f32[32,1,1128]{2,1,0:T(1,128)S(1)} all-to-all(f32[32,1,1128]{2,1,0:T(1,128)S(1)} %broadcast_in_dim.29), channel_id=1, replica_groups=mesh['sec'=4,'wide'=8] {'sec','wide'}, dimensions={0} | all-to-all | bytes 288768 | tf_op jit(solution)/shard_map/all_to_all | solution.py:213
  40.4 0.0 copy-done.1
  40.4 6.8 %update.1 = (bf16[1000,2048]{1,0:T(8,128)(2,1)}, f32[4,1000]{1,0:T(4,128)}) custom-call(s32[1]{0:T(128)} %bitcast.pos_ref, f32[32,1,1128]{2,1,0:T(1,128)S(1)} %all_to_all.15.both_ref, f32[1,128]{1,0:T(1,128)S(1)} %bitcast.11, bf16[32,2048]{1,0:T(8,128)(2,1)S(1)} %get-tuple-element.13.kern_ref, f32[2048,128]{1,0:T(8,128)S(1)} %get-tuple-element.11.vecs_ref, ...), custom_call_target="tpu_custom_call" | custom-call | tf_op jit(solution)/shard_map/update/pallas_call | solution.py:217
  (5 shorter events, 0.0 us)
Async XLA Ops:
  0.6 20.9 %copy-start = (f32[64,1000]{1,0:T(8,128)S(1)}, f32[64,1000]{1,0:T(8,128)}, u32[]{:S(2)}) copy-start(f32[64,1000]{1,0:T(8,128)} %param.9) | copy-start | bytes 768004
  2.3 12.1 %all-to-all-start = ((bf16[8,4,512]{2,1,0:T(4,128)(2,1)}), bf16[8,4,512]{2,1,0:T(4,128)(2,1)S(1)}, u32[]{:S(2)}, u32[]{:S(2)}) async-start(bf16[8,4,512]{2,1,0:T(4,128)(2,1)} %gather.7), calls=%async_computation | async-start | bytes 65536 | tf_op jit(solution)/shard_map/all_to_all | solution.py:168
  11.6 9.9 %copy-start.2 = (s32[4]{0:T(128)S(1)}, s32[4]{0:T(128)}, u32[]{:S(2)}) copy-start(s32[4]{0:T(128)} %idx_hbm.1) | copy-start | bytes 52
  14.4 26.0 %copy-start.1 = (f32[128]{0:T(128)S(1)}, f32[128]{0:T(128)}, u32[]{:S(2)}) copy-start(f32[128]{0:T(128)} %param.15) | copy-start | bytes 1540
  18.1 11.7 %all-to-all-start.1 = ((f32[32,1,1128]{2,1,0:T(1,128)}), f32[32,1,1128]{2,1,0:T(1,128)S(1)}, u32[]{:S(2)}, u32[]{:S(2)}) async-start(f32[32,1,1128]{2,1,0:T(1,128)} %get-tuple-element.12), calls=%async_computation.1 | async-start | bytes 294912 | tf_op jit(solution)/shard_map/all_to_all | solution.py:211

commit v4 on v3

v4 whole, which is shorter than its diff:
```python
import functools
import math

import jax
import jax.numpy as jnp
from jax import lax
from jax.experimental import pallas as pl
from jax.experimental.pallas import tpu as pltpu
from jax.sharding import PartitionSpec as P

LANES = 128
VMEM_GRANT = 16 << 20
NT = (((1,), (1,)), ((), ()))
NN = (((1,), (0,)), ((), ()))


def dot32(a, b, dims):
    return lax.dot_general(a, b, dims, preferred_element_type=jnp.float32)


def halves(x):
    top = x.astype(jnp.bfloat16)
    return top, (x - top.astype(jnp.float32)).astype(jnp.bfloat16)


def in_hbm(x):
    return pltpu.with_memory_space_constraint(x, pltpu.HBM)


def gather_body(pos_ref, idx_hbm, rows_hbm, out_ref, idx_ref, rows_ref, sems):
    get_idx = pltpu.make_async_copy(idx_hbm, idx_ref, sems.at[0])
    get_rows = pltpu.make_async_copy(rows_hbm, rows_ref, sems.at[1])
    get_idx.start()
    get_rows.start()
    get_idx.wait()
    pool_rows = rows_ref.shape[0]
    copies, batch_rows = out_ref.shape[:2]
    shape = (batch_rows, pool_rows)
    row = lax.broadcasted_iota(jnp.int32, shape, 0)
    wanted = jnp.zeros(shape, jnp.int32)
    for j in range(batch_rows):
        wanted = jnp.where(row == j, idx_ref[j] - pos_ref[0] * pool_rows, wanted)
    picked = (lax.broadcasted_iota(jnp.int32, shape, 1) == wanted).astype(jnp.bfloat16)
    get_rows.wait()
    rows = dot32(picked, rows_ref[...], NN).astype(jnp.bfloat16)
    for w in range(copies):
        out_ref[w] = rows


def stage_body(
    pos_ref, nys_hbm, eig_hbm, idx_hbm, targets_hbm, cents_hbm, cents_ref, cent_sq_ref, vecs_ref, wanted_ref,
    nys_ref, eig_ref, idx_ref, targets_ref, sems, *, wide_count
):
    pairs = (
        (nys_hbm, nys_ref), (eig_hbm, eig_ref), (idx_hbm, idx_ref), (targets_hbm, targets_ref), (cents_hbm, cents_ref)
    )
    gets = [pltpu.make_async_copy(src, dst, sems.at[i]) for i, (src, dst) in enumerate(pairs)]
    for get in gets:
        get.start()
    gets[0].wait()
    gets[1].wait()
    center_rows, feat_dim = cents_ref.shape
    nys_count, eig_count = eig_ref.shape
    eig_both = jnp.concatenate(halves(eig_ref[...]), axis=1)
    place = nys_ref[...] - pos_ref[0] * center_rows
    for start in range(0, center_rows, LANES):
        rows = pl.ds(start, LANES)
        at = lax.broadcasted_iota(jnp.int32, (LANES, nys_count), 0) + start
        moved = dot32((at == place).astype(jnp.bfloat16), eig_both, NN)
        vec_hi, vec_lo = halves(moved[:, :eig_count] + moved[:, eig_count:])
        vecs_ref[rows, :eig_count] = vec_hi
        vecs_ref[rows, eig_count:] = vec_lo
    gets[2].wait()
    gets[3].wait()
    pool_rows, classes = targets_ref.shape
    row = idx_ref[pos_ref[0] // wide_count] - pos_ref[0] % wide_count * pool_rows
    wanted_ref[...] = jnp.zeros_like(wanted_ref)
    wanted_ref[:, pl.ds(eig_count, classes)] = targets_ref[pl.ds(row, 1), :]
    gets[4].wait()
    for start in range(0, center_rows, LANES):
        total = jnp.zeros((LANES, LANES), jnp.float32)
        for lane in range(0, feat_dim, LANES):
            part = cents_ref[pl.ds(start, LANES), pl.ds(lane, LANES)].astype(jnp.float32)
            total = total + part * part
        cent_sq_ref[:, pl.ds(start, LANES)] = jnp.sum(total.T, axis=0, keepdims=True)


def fetch(src_hbm, dst_ref, sems, step):
    gets = []
    for i in range(src_hbm.shape[1] // step):
        cols = pl.ds(i * step, step)
        gets.append(pltpu.make_async_copy(src_hbm.at[:, cols], dst_ref.at[:, cols], sems.at[i]))
        gets[-1].start()
    return gets


def lanes(ref, row, count, tile, tiles):
    return ref.at[pl.ds(row * tiles + tile, count, stride=tiles), :]


def share_body(pos_ref, feats_ref, cents_ref, cent_sq_ref, vecs_ref, wt_hbm, kern_ref, part_ref, wt_ref, sems, *, step):
    gets = fetch(wt_hbm, wt_ref, sems, step)

    @pl.when(pos_ref[0] >= 0)
    def _():
        batch_total = feats_ref.shape[0]
        center_rows, feat_dim = cents_ref.shape
        classes = wt_ref.shape[0]
        eig_count = vecs_ref.shape[1] // 2
        tiles = part_ref.shape[0] // batch_total
        length = 1.5 / math.sqrt(feat_dim)
        feats = feats_ref[...]
        wide_feats = feats.astype(jnp.float32)
        row_sq = jnp.sum(wide_feats * wide_feats, axis=1, keepdims=True)
        for start in range(0, center_rows, step):
            cols = pl.ds(start, step)
            cross = dot32(feats, cents_ref[cols, :], NT)
            dist_sq = jnp.maximum(row_sq + cent_sq_ref[:, cols] - 2.0 * cross, 0.0)
            kern_ref[:, cols] = jnp.exp((1.4142 - jnp.sqrt(dist_sq)) / length).astype(jnp.bfloat16)
        coords = dot32(kern_ref[...], vecs_ref[...], NN)
        coords = coords[:, :eig_count] + coords[:, eig_count:]
        total = None
        for i, get in enumerate(gets):
            cols = pl.ds(i * step, step)
            get.wait()
            term = dot32(kern_ref[:, cols], wt_ref[:, cols], NT)
            total = term if total is None else total + term
        pad = jnp.zeros((batch_total, tiles * LANES - eig_count - classes), jnp.float32)
        part = jnp.concatenate([coords, total, pad], axis=1)
        for tile in range(tiles):
            for row in range(0, batch_total, 8):
                lanes(part_ref, row, 8, tile, tiles)[...] = part[row : row + 8, tile * LANES : (tile + 1) * LANES]


def update_body(
    pos_ref, both_ref, scale_ref, kern_ref, vecs_ref, wt_hbm, out_hbm, res_ref,
    left_ref, wt_ref, new_ref, get_sems, put_sems, *, rate, sections, step, chunk
):
    gets = fetch(wt_hbm, wt_ref, get_sems, step)
    fold = math.frexp(rate)[0] == 0.5
    classes = wt_ref.shape[0]
    batch_total = kern_ref.shape[0]
    eig_count = vecs_ref.shape[1] // 2
    first = eig_count // LANES
    tiles = both_ref.shape[0] // batch_total
    wide_count = batch_total // sections
    for tile in range(first, tiles):
        rows = lanes(both_ref, 0, batch_total, tile, tiles)[...].astype(jnp.bfloat16)
        if fold:
            rows = (rows.astype(jnp.float32) * rate).astype(jnp.bfloat16)
        turned = jnp.concatenate([rows, rows, rows, rows], axis=0).T
        left_ref[pl.ds((tile - first) * LANES, LANES), :] = turned
    coords = jnp.concatenate([lanes(both_ref, 0, batch_total, tile, tiles)[...] for tile in range(first)], axis=1)
    coords_hi, coords_lo = halves(coords * scale_ref[...])
    both_hi = jnp.concatenate([coords_hi, coords_hi], axis=1)
    puts = []
    for i, get in enumerate(gets):
        cols = pl.ds(i * step, step)
        vecs = vecs_ref[cols, :]
        drop = dot32(both_hi, vecs, NT) + dot32(coords_lo, vecs[:, :eig_count], NT)
        drop_hi, drop_lo = halves(-drop)
        factors = jnp.concatenate([kern_ref[:, cols], drop_hi, drop_lo, jnp.zeros_like(drop_lo)], axis=0)
        get.wait()
        for row in range(0, classes, chunk):
            part = pl.ds(row, min(chunk, classes - row))
            grad = dot32(left_ref[part, :], factors, NN)
            grad = grad if fold else rate * grad
            new_ref[part, cols] = (wt_ref[part, cols].astype(jnp.float32) - grad).astype(jnp.bfloat16)
        puts.append(pltpu.make_async_copy(new_ref.at[:, cols], out_hbm.at[:, cols], put_sems.at[i]))
        puts[-1].start()
    for s in range(sections):
        for tile in range(first, tiles):
            width = min(LANES, classes - (tile - first) * LANES)
            row = lanes(both_ref, s * wide_count + pos_ref[0], 1, tile, tiles)[...]
            res_ref[pl.ds(s, 1), pl.ds((tile - first) * LANES, width)] = row[:, :width]
    for put in puts:
        put.wait()


def shards(train_feats, train_targets, batch_idx, centers, weights, nys_idx, eig_vecs, eig_scale):
    batch_rows = batch_idx.shape[0]
    center_rows, feat_dim = centers.shape
    classes = weights.shape[1]
    eig_count = eig_vecs.shape[1]
    wide_count = lax.axis_size("wide")
    sec_count = lax.axis_size("sec")
    wide_pos = lax.axis_index("wide")
    sec_pos = lax.axis_index("sec")
    batch_total = batch_rows * wide_count
    tiles = eig_count // LANES + pl.cdiv(classes, LANES)
    assert batch_rows == sec_count and eig_count % LANES == 0
    vmem = pl.BlockSpec(memory_space=pltpu.VMEM)
    smem = pl.BlockSpec(memory_space=pltpu.SMEM)
    hbm = pl.BlockSpec(memory_space=pltpu.HBM)

    params = pltpu.CompilerParams(vmem_limit_bytes=VMEM_GRANT)
    step = min(512, center_rows)

    copies = pl.pallas_call(
        gather_body,
        out_shape=jax.ShapeDtypeStruct((wide_count, batch_rows, feat_dim), jnp.bfloat16),
        in_specs=[smem, hbm, hbm],
        out_specs=vmem,
        scratch_shapes=[
            pltpu.SMEM((batch_rows,), jnp.int32),
            pltpu.VMEM(train_feats.shape, train_feats.dtype),
            pltpu.SemaphoreType.DMA((2,)),
        ],
        compiler_params=params,
        name="gather",
    )(wide_pos[None], in_hbm(batch_idx), in_hbm(train_feats))
    piece = lax.all_to_all(copies, "wide", 0, 0, tiled=False)
    piece = jnp.transpose(piece, (1, 0, 2)).reshape(batch_total, feat_dim)

    turned_weights = in_hbm(weights.T)
    staged_centers, cent_sq, vecs, wanted = pl.pallas_call(
        functools.partial(stage_body, wide_count=wide_count),
        out_shape=(
            jax.ShapeDtypeStruct(centers.shape, centers.dtype),
            jax.ShapeDtypeStruct((1, center_rows), jnp.float32),
            jax.ShapeDtypeStruct((center_rows, 2 * eig_count), jnp.bfloat16),
            jax.ShapeDtypeStruct((1, tiles * LANES), jnp.float32),
        ),
        in_specs=[smem] + [hbm] * 5,
        out_specs=(vmem,) * 4,
        scratch_shapes=[
            pltpu.VMEM((1, nys_idx.shape[0]), jnp.int32),
            pltpu.VMEM(eig_vecs.shape, jnp.float32),
            pltpu.SMEM((batch_rows,), jnp.int32),
            pltpu.VMEM(train_targets.shape, jnp.float32),
            pltpu.SemaphoreType.DMA((5,)),
        ],
        compiler_params=params,
        cost_estimate=pl.CostEstimate(flops=1 << 31, bytes_accessed=16 << 20, transcendentals=0),
        name="stage",
    )(
        (sec_pos * wide_count + wide_pos)[None],
        in_hbm(nys_idx[None, :]),
        in_hbm(eig_vecs),
        in_hbm(batch_idx),
        in_hbm(train_targets),
        in_hbm(centers),
    )

    slabs = center_rows // step
    kern, part = pl.pallas_call(
        functools.partial(share_body, step=step),
        out_shape=(
            jax.ShapeDtypeStruct((batch_total, center_rows), jnp.bfloat16),
            jax.ShapeDtypeStruct((batch_total * tiles, LANES), jnp.float32),
        ),
        in_specs=[smem] + [vmem] * 4 + [hbm],
        out_specs=(vmem, vmem),
        scratch_shapes=[pltpu.VMEM((classes, center_rows), jnp.bfloat16), pltpu.SemaphoreType.DMA((slabs,))],
        compiler_params=params,
        name="share",
    )(wide_pos[None], piece, staged_centers, cent_sq, vecs, turned_weights)

    part = lax.all_to_all(part.reshape(batch_total, 1, tiles * LANES), ("sec", "wide"), 0, 0, tiled=False)
    mine = jnp.sum(part, axis=0) - wanted
    both = lax.all_to_all(jnp.broadcast_to(mine[None], part.shape), ("sec", "wide"), 0, 0, tiled=False)
    both = both.reshape(batch_total * tiles, LANES)

    new_turned, residual = pl.pallas_call(
        functools.partial(update_body, rate=16.0 / batch_total, sections=sec_count, step=step, chunk=128),
        out_shape=(
            jax.ShapeDtypeStruct((classes, center_rows), jnp.bfloat16),
            jax.ShapeDtypeStruct((batch_rows, classes), jnp.float32),
        ),
        in_specs=[smem] + [vmem] * 4 + [hbm],
        out_specs=(hbm, vmem),
        scratch_shapes=[
            pltpu.VMEM((pl.cdiv(classes, LANES) * LANES, 4 * batch_total), jnp.bfloat16),
            pltpu.VMEM((classes, center_rows), jnp.bfloat16),
            pltpu.VMEM((classes, center_rows), jnp.bfloat16),
            pltpu.SemaphoreType.DMA((slabs,)),
            pltpu.SemaphoreType.DMA((slabs,)),
        ],
        compiler_params=params,
        name="update",
    )(wide_pos[None], both, eig_scale[None, :], kern, vecs, turned_weights)
    return (new_turned.T, residual)


def solution(mesh):
    return jax.shard_map(
        shards,
        mesh=mesh,
        in_specs=(
            P("wide", None),
            P("wide", None),
            P("wide"),
            P(("sec", "wide"), None),
            P(("sec", "wide"), None),
            P("wide"),
            P("wide", None),
            P(),
        ),
        out_specs=(P(("sec", "wide"), None), P("wide", None)),
        check_vma=False,
    )
```

time: 47.6 us -> 44.2 us (0.929)
  blocking collectives: 10.2 us -> 21.2 us
  waiting for transfers between devices: 10.5 us -> 3.44 us
  starting transfers between devices: 9.7 us -> 6.37 us
  Pallas kernels: 15.2 us -> 11.9 us
  local copies, waits for them, and re-layouts: 0.75 us -> 0.09 us
    all_to_all x1 -> x2, blocking collectives: 10.2 us -> 21.2 us  [the longest x1 11.1 us: shards(): lax.all_to_all(part.reshape(batch_total, 1, tiles * LANES), ('sec', 'wide...]
    all_to_all x1 -> x0, waiting for transfers between devices: 7.74 us -> none  [shards(): lax.all_to_all(part, ('sec', 'wide'), 0, 0, tiled=False)]
    all_to_all x1 -> x0, starting transfers between devices: 3.33 us -> none  [shards(): lax.all_to_all(part, ('sec', 'wide'), 0, 0, tiled=False)]
    pallas_call x1, Pallas kernels: 6.85 us -> 4.77 us  [shards(): pl.pallas_call(functools.partial(update_body, rate=16.0 / batch_total, se...]
    all_to_all x1, waiting for transfers between devices: 2.76 us -> 3.44 us  [shards(): piece = lax.all_to_all(copies, 'wide', 0, 0, tiled=False)]
    pallas_call x1, Pallas kernels: 2.96 us -> 2.29 us  [shards(): pl.pallas_call(functools.partial(stage_body, wide_count=wide_count), out_...]
    gather x1 -> x0, local copies, waits for them, and re-layouts: 0.57 us -> none  [shards(): train_targets[batch_idx - wide_pos * pool_rows]]
  transfers between devices with their start and end apart: 2 -> 1, of which waited for: 2 -> 1; matrix products, arithmetic and copies ran while one was open for 1% -> 0% of each run, Pallas kernels for 6% -> 5%
where the time goes in v4:
time: 44.2 us; the launch traced here: 43.9 us
  blocking collectives  21.2 us (48%)
  Pallas kernels  11.9 us (27%)
  starting transfers between devices  6.37 us (14%)
  waiting for transfers between devices  3.44 us (8%)
  between operations  0.68 us (2%)
    all_to_all x1, blocking collectives, shards(): lax.all_to_all(part.reshape(batch_total, 1, tiles * LANES), ('sec', 'wide...  11.1 us
    all_to_all x1, blocking collectives, shards(): lax.all_to_all(jnp.broadcast_to(mine[None], part.shape), ('sec', 'wide'),...  10.2 us
    all_to_all x1, starting transfers between devices, shards(): piece = lax.all_to_all(copies, 'wide', 0, 0, tiled=False)  6.37 us
    pallas_call x1, Pallas kernels, shards(): pl.pallas_call(functools.partial(update_body, rate=16.0 / batch_total, se...  4.77 us
    all_to_all x1, waiting for transfers between devices, shards(): piece = lax.all_to_all(copies, 'wide', 0, 0, tiled=False)  3.44 us
    pallas_call x1, Pallas kernels, shards(): pl.pallas_call(functools.partial(share_body, step=step), out_shape=(jax.S...  3.24 us
    pallas_call x1, Pallas kernels, shards(): pl.pallas_call(functools.partial(stage_body, wide_count=wide_count), out_...  2.29 us
    pallas_call x1, Pallas kernels, shards(): pl.pallas_call(gather_body, out_shape=jax.ShapeDtypeStruct((wide_count, b...  1.6 us
  transfers between devices with their start and end apart: 1, of which 1 were waited for; matrix products, arithmetic and copies ran while one was open for 0% of the time, Pallas kernels for 5%

profile of v4, /device:TPU:0, one launch (start us, length us, event | category | flops | bytes accessed | tf_op | source)
XLA Modules:
  0.0 43.9 jit_solution(14456472320401054205)
XLA Ops:
  0.6 1.6 %gather.1 = bf16[8,4,512]{2,1,0:T(4,128)(2,1)} custom-call(s32[1]{0:T(128)} %bitcast.pos_ref, s32[4]{0:T(128)} %idx_hbm.3, bf16[64,512]{1,0:T(8,128)(2,1)} %rows_hbm.1), custom_call_target="tpu_custom_call" | custom-call | tf_op jit(solution)/shard_map/gather/pallas_call | solution.py:199
  2.2 6.4 %all-to-all-start = ((bf16[8,4,512]{2,1,0:T(4,128)(2,1)}), bf16[8,4,512]{2,1,0:T(4,128)(2,1)S(1)}, u32[]{:S(2)}, u32[]{:S(2)}) async-start(bf16[8,4,512]{2,1,0:T(4,128)(2,1)} %gather.1), calls=%async_computation | async-start | bytes 65536 | tf_op jit(solution)/shard_map/all_to_all | solution.py:212
  8.6 2.3 %stage.1 = (bf16[2048,512]{1,0:T(8,128)(2,1)S(1)}, f32[1,2048]{1,0:T(1,128)S(1)}, bf16[2048,256]{1,0:T(8,128)(2,1)S(1)}, f32[1,1152]{1,0:T(1,128)S(1)}) custom-call(s32[1]{0:T(128)} %bitcast.3.pos_ref, s32[1,256]{1,0:T(1,128)} %bitcast.20, f32[256,128]{1,0:T(8,128)} %eig_hbm.1, s32[4]{0:T(128)} %idx_hbm.3, f32[64,1000]{1,0:T(8,128)} %targets_hbm.1, ...), custom_call_target="tpu_custom_call" | custom-call | flops 2147483648 | bytes 16777216 | tf_op jit(solution)/shard_map/stage/pallas_call | solution.py:216
  10.9 3.4 %all-to-all-done = bf16[8,4,512]{2,1,0:T(4,128)(2,1)S(1)} async-done(((bf16[8,4,512]{2,1,0:T(4,128)(2,1)}), bf16[8,4,512]{2,1,0:T(4,128)(2,1)S(1)}, u32[]{:S(2)}, u32[]{:S(2)}) %all-to-all-start) | async-done | bytes 32800 | tf_op jit(solution)/shard_map/all_to_all | solution.py:212
  14.4 0.0 copy-start
  14.4 3.2 %share.1 = (bf16[32,2048]{1,0:T(8,128)(2,1)S(1)}, f32[288,128]{1,0:T(8,128)S(1)}) custom-call(s32[1]{0:T(128)} %bitcast.pos_ref, bf16[32,512]{1,0:T(8,128)(2,1)S(1)} %bitcast.14, bf16[2048,512]{1,0:T(8,128)(2,1)S(1)} %get-tuple-element.10.cents_ref, f32[1,2048]{1,0:T(1,128)S(1)} %get-tuple-element.11.cent_sq_ref, ...), custom_call_target="tpu_custom_call" | custom-call | tf_op jit(solution)/shard_map/share/pallas_call | solution.py:246
  17.6 11.1 %all_to_all.15 = f32[32,1,1152]{2,1,0:T(1,128)S(1)} all-to-all(f32[32,1,1152]{2,1,0:T(1,128)S(1)} %bitcast.13), channel_id=1, replica_groups=mesh['sec'=4,'wide'=8] {'sec','wide'}, dimensions={0} | all-to-all | bytes 294912 | tf_op jit(solution)/shard_map/all_to_all | solution.py:259
  28.7 0.1 reduce_sum.11
  28.8 0.1 broadcast_in_dim.26
  28.9 10.2 %all_to_all.16 = f32[32,1,1152]{2,1,0:T(1,128)S(1)} all-to-all(f32[32,1,1152]{2,1,0:T(1,128)S(1)} %broadcast_in_dim.26), channel_id=1, replica_groups=mesh['sec'=4,'wide'=8] {'sec','wide'}, dimensions={0} | all-to-all | bytes 294912 | tf_op jit(solution)/shard_map/all_to_all | solution.py:261
  39.1 0.0 copy-done
  39.1 4.8 %update.1 = (bf16[1000,2048]{1,0:T(8,128)(2,1)}, f32[4,1000]{1,0:T(4,128)}) custom-call(s32[1]{0:T(128)} %bitcast.pos_ref, f32[288,128]{1,0:T(8,128)S(1)} %bitcast.12, f32[1,128]{1,0:T(1,128)S(1)} %bitcast.15, bf16[32,2048]{1,0:T(8,128)(2,1)S(1)} %get-tuple-element.15.kern_ref, bf16[2048,256]{1,0:T(8,128)(2,1)S(1)} %get-tuple-element.12.vecs_ref, ...), custom_call_target="tpu_custom_call" | custom-call | tf_op jit(solution)/shard_map/update/pallas_call | solution.py:264
  (2 shorter events, 0.0 us)
Async XLA Ops:
  2.2 12.1 %all-to-all-start = ((bf16[8,4,512]{2,1,0:T(4,128)(2,1)}), bf16[8,4,512]{2,1,0:T(4,128)(2,1)S(1)}, u32[]{:S(2)}, u32[]{:S(2)}) async-start(bf16[8,4,512]{2,1,0:T(4,128)(2,1)} %gather.1), calls=%async_computation | async-start | bytes 65536 | tf_op jit(solution)/shard_map/all_to_all | solution.py:212
  14.4 24.7 %copy-start = (f32[128]{0:T(128)S(1)}, f32[128]{0:T(128)}, u32[]{:S(2)}) copy-start(f32[128]{0:T(128)} %param.15) | copy-start | bytes 1540

commit v5 on v4

--- a/solution.py
+++ b/solution.py
@@ -85,21 +85,16 @@
         cent_sq_ref[:, pl.ds(start, LANES)] = jnp.sum(total.T, axis=0, keepdims=True)
 
 
-def fetch(src_hbm, dst_ref, sems, step):
-    gets = []
-    for i in range(src_hbm.shape[1] // step):
-        cols = pl.ds(i * step, step)
-        gets.append(pltpu.make_async_copy(src_hbm.at[:, cols], dst_ref.at[:, cols], sems.at[i]))
-        gets[-1].start()
-    return gets
-
-
 def lanes(ref, row, count, tile, tiles):
     return ref.at[pl.ds(row * tiles + tile, count, stride=tiles), :]
 
 
 def share_body(pos_ref, feats_ref, cents_ref, cent_sq_ref, vecs_ref, wt_hbm, kern_ref, part_ref, wt_ref, sems, *, step):
-    gets = fetch(wt_hbm, wt_ref, sems, step)
+    gets = []
+    for i in range(wt_hbm.shape[1] // step):
+        cols = pl.ds(i * step, step)
+        gets.append(pltpu.make_async_copy(wt_hbm.at[:, cols], wt_ref.at[:, cols], sems.at[i]))
+        gets[-1].start()
 
     @pl.when(pos_ref[0] >= 0)
     def _():
@@ -132,11 +127,18 @@
                 lanes(part_ref, row, 8, tile, tiles)[...] = part[row : row + 8, tile * LANES : (tile + 1) * LANES]
 
 
+def settle_body(parts_ref, wanted_ref, both_ref, *, count):
+    tiles = parts_ref.shape[0] // count
+    for tile in range(tiles):
+        total = jnp.sum(lanes(parts_ref, 0, count, tile, tiles)[...], axis=0, keepdims=True)
+        total = total - wanted_ref[:, tile * LANES : (tile + 1) * LANES]
+        lanes(both_ref, 0, count, tile, tiles)[...] = jnp.broadcast_to(total, (count, LANES))
+
+
 def update_body(
-    pos_ref, both_ref, scale_ref, kern_ref, vecs_ref, wt_hbm, out_hbm, res_ref,
-    left_ref, wt_ref, new_ref, get_sems, put_sems, *, rate, sections, step, chunk
+    pos_ref, both_ref, scale_ref, kern_ref, vecs_ref, wt_ref, out_hbm, res_hbm,
+    left_ref, factors_ref, new_ref, res_ref, sems, *, rate, sections, step, chunk
 ):
-    gets = fetch(wt_hbm, wt_ref, get_sems, step)
     fold = math.frexp(rate)[0] == 0.5
     classes = wt_ref.shape[0]
     batch_total = kern_ref.shape[0]
@@ -152,27 +154,36 @@
         left_ref[pl.ds((tile - first) * LANES, LANES), :] = turned
     coords = jnp.concatenate([lanes(both_ref, 0, batch_total, tile, tiles)[...] for tile in range(first)], axis=1)
     coords_hi, coords_lo = halves(coords * scale_ref[...])
-    both_hi = jnp.concatenate([coords_hi, coords_hi], axis=1)
+    coords = jnp.concatenate([coords_hi, coords_lo], axis=0)
+    coords = jnp.concatenate([coords, coords], axis=1)
+    for start in range(0, wt_ref.shape[1], step):
+        cols = pl.ds(start, step)
+        drop = dot32(coords, vecs_ref[cols, :], NT)
+        drop = drop[:batch_total] + drop[batch_total:]
+        drop_hi, drop_lo = halves(-drop)
+        factors_ref[:, cols] = jnp.concatenate([kern_ref[:, cols], drop_hi, drop_lo, jnp.zeros_like(drop_lo)], axis=0)
     puts = []
-    for i, get in enumerate(gets):
-        cols = pl.ds(i * step, step)
-        vecs = vecs_ref[cols, :]
-        drop = dot32(both_hi, vecs, NT) + dot32(coords_lo, vecs[:, :eig_count], NT)
-        drop_hi, drop_lo = halves(-drop)
-        factors = jnp.concatenate([kern_ref[:, cols], drop_hi, drop_lo, jnp.zeros_like(drop_lo)], axis=0)
-        get.wait()
+    for start in range(0, wt_ref.shape[1], step):
+        cols = pl.ds(start, step)
+        factors = factors_ref[:, cols]
         for row in range(0, classes, chunk):
             part = pl.ds(row, min(chunk, classes - row))
             grad = dot32(left_ref[part, :], factors, NN)
             grad = grad if fold else rate * grad
             new_ref[part, cols] = (wt_ref[part, cols].astype(jnp.float32) - grad).astype(jnp.bfloat16)
-        puts.append(pltpu.make_async_copy(new_ref.at[:, cols], out_hbm.at[:, cols], put_sems.at[i]))
-        puts[-1].start()
-    for s in range(sections):
-        for tile in range(first, tiles):
-            width = min(LANES, classes - (tile - first) * LANES)
-            row = lanes(both_ref, s * wide_count + pos_ref[0], 1, tile, tiles)[...]
-            res_ref[pl.ds(s, 1), pl.ds((tile - first) * LANES, width)] = row[:, :width]
+            if row // chunk % 2 == 1 or row + chunk >= classes:
+                rows = pl.ds(row // chunk // 2 * 2 * chunk, row % (2 * chunk) + part.size)
+                spot = (rows, cols)
+                puts.append(pltpu.make_async_copy(new_ref.at[spot], out_hbm.at[spot], sems.at[len(puts)]))
+                puts[-1].start()
+        if start == 0:
+            for s in range(sections):
+                for tile in range(first, tiles):
+                    width = min(LANES, classes - (tile - first) * LANES)
+                    row = lanes(both_ref, s * wide_count + pos_ref[0], 1, tile, tiles)[...]
+                    res_ref[pl.ds(s, 1), pl.ds((tile - first) * LANES, width)] = row[:, :width]
+            puts.append(pltpu.make_async_copy(res_ref, res_hbm, sems.at[len(puts)]))
+            puts[-1].start()
     for put in puts:
         put.wait()
 
@@ -194,7 +205,8 @@
     hbm = pl.BlockSpec(memory_space=pltpu.HBM)
 
     params = pltpu.CompilerParams(vmem_limit_bytes=VMEM_GRANT)
-    step = min(512, center_rows)
+    step = min(512, center_rows // 4)
+    chunk = LANES
 
     copies = pl.pallas_call(
         gather_body,
@@ -242,43 +254,51 @@
         in_hbm(centers),
     )
 
-    slabs = center_rows // step
-    kern, part = pl.pallas_call(
+    slab_count = center_rows // step
+    kern, part, kept = pl.pallas_call(
         functools.partial(share_body, step=step),
         out_shape=(
             jax.ShapeDtypeStruct((batch_total, center_rows), jnp.bfloat16),
             jax.ShapeDtypeStruct((batch_total * tiles, LANES), jnp.float32),
+            jax.ShapeDtypeStruct((classes, center_rows), jnp.bfloat16),
         ),
         in_specs=[smem] + [vmem] * 4 + [hbm],
-        out_specs=(vmem, vmem),
-        scratch_shapes=[pltpu.VMEM((classes, center_rows), jnp.bfloat16), pltpu.SemaphoreType.DMA((slabs,))],
+        out_specs=(vmem, vmem, vmem),
+        scratch_shapes=[pltpu.SemaphoreType.DMA((slab_count,))],
         compiler_params=params,
         name="share",
     )(wide_pos[None], piece, staged_centers, cent_sq, vecs, turned_weights)
 
-    part = lax.all_to_all(part.reshape(batch_total, 1, tiles * LANES), ("sec", "wide"), 0, 0, tiled=False)
-    mine = jnp.sum(part, axis=0) - wanted
-    both = lax.all_to_all(jnp.broadcast_to(mine[None], part.shape), ("sec", "wide"), 0, 0, tiled=False)
+    parts = lax.all_to_all(part.reshape(batch_total, 1, tiles * LANES), ("sec", "wide"), 0, 0, tiled=False)
+    both = pl.pallas_call(
+        functools.partial(settle_body, count=batch_total),
+        out_shape=jax.ShapeDtypeStruct((batch_total * tiles, LANES), jnp.float32),
+        in_specs=[vmem, vmem],
+        out_specs=vmem,
+        compiler_params=params,
+        name="settle",
+    )(parts.reshape(batch_total * tiles, LANES), wanted)
+    both = lax.all_to_all(both.reshape(batch_total, 1, tiles * LANES), ("sec", "wide"), 0, 0, tiled=False)
     both = both.reshape(batch_total * tiles, LANES)
 
     new_turned, residual = pl.pallas_call(
-        functools.partial(update_body, rate=16.0 / batch_total, sections=sec_count, step=step, chunk=128),
+        functools.partial(update_body, rate=16.0 / batch_total, sections=sec_count, step=step, chunk=chunk),
         out_shape=(
             jax.ShapeDtypeStruct((classes, center_rows), jnp.bfloat16),
             jax.ShapeDtypeStruct((batch_rows, classes), jnp.float32),
         ),
-        in_specs=[smem] + [vmem] * 4 + [hbm],
-        out_specs=(hbm, vmem),
+        in_specs=[smem] + [vmem] * 5,
+        out_specs=(hbm, hbm),
         scratch_shapes=[
             pltpu.VMEM((pl.cdiv(classes, LANES) * LANES, 4 * batch_total), jnp.bfloat16),
+            pltpu.VMEM((4 * batch_total, center_rows), jnp.bfloat16),
             pltpu.VMEM((classes, center_rows), jnp.bfloat16),
-            pltpu.VMEM((classes, center_rows), jnp.bfloat16),
-            pltpu.SemaphoreType.DMA((slabs,)),
-            pltpu.SemaphoreType.DMA((slabs,)),
+            pltpu.VMEM((batch_rows, classes), jnp.float32),
+            pltpu.SemaphoreType.DMA((1 + slab_count * pl.cdiv(classes, 2 * chunk),)),
         ],
         compiler_params=params,
         name="update",
-    )(wide_pos[None], both, eig_scale[None, :], kern, vecs, turned_weights)
+    )(wide_pos[None], both, eig_scale[None, :], kern, vecs, kept)
     return (new_turned.T, residual)
 
 

time: 44.2 us -> 41.8 us (0.946)
  Pallas kernels: 11.9 us -> 9.79 us
    pallas_call x1, Pallas kernels: 4.77 us -> 2.64 us  [shards(): pl.pallas_call(functools.partial(update_body, rate=16.0 / batch_total, se...]
  transfers between devices with their start and end apart: 1 -> 1, of which waited for: 1 -> 1; matrix products, arithmetic and copies ran while one was open for 0% -> 0% of each run, Pallas kernels for 5% -> 6%
where the time goes in v5:
time: 41.8 us; the launch traced here: 41.5 us
  blocking collectives  21.2 us (51%)
  Pallas kernels  9.79 us (23%)
  starting transfers between devices  6.37 us (15%)
  waiting for transfers between devices  3.44 us (8%)
  between operations  0.67 us (2%)
    all_to_all x1, blocking collectives, shards(): lax.all_to_all(part.reshape(batch_total, 1, tiles * LANES), ('sec', 'wide...  11.1 us
    all_to_all x1, blocking collectives, shards(): lax.all_to_all(both.reshape(batch_total, 1, tiles * LANES), ('sec', 'wide...  10.2 us
    all_to_all x1, starting transfers between devices, shards(): piece = lax.all_to_all(copies, 'wide', 0, 0, tiled=False)  6.37 us
    all_to_all x1, waiting for transfers between devices, shards(): piece = lax.all_to_all(copies, 'wide', 0, 0, tiled=False)  3.44 us
    pallas_call x1, Pallas kernels, shards(): pl.pallas_call(functools.partial(share_body, step=step), out_shape=(jax.S...  3.24 us
    pallas_call x1, Pallas kernels, shards(): pl.pallas_call(functools.partial(update_body, rate=16.0 / batch_total, se...  2.64 us
    pallas_call x1, Pallas kernels, shards(): pl.pallas_call(functools.partial(stage_body, wide_count=wide_count), out_...  2.29 us
    pallas_call x1, Pallas kernels, shards(): pl.pallas_call(gather_body, out_shape=jax.ShapeDtypeStruct((wide_count, b...  1.6 us
  transfers between devices with their start and end apart: 1, of which 1 were waited for; matrix products, arithmetic and copies ran while one was open for 0% of the time, Pallas kernels for 6%

profile of v5, /device:TPU:0, one launch (start us, length us, event | category | flops | bytes accessed | tf_op | source)
XLA Modules:
  0.0 41.5 jit_solution(1515223171021187483)
XLA Ops:
  0.6 1.6 %gather.1 = bf16[8,4,512]{2,1,0:T(4,128)(2,1)} custom-call(s32[1]{0:T(128)} %bitcast.pos_ref, s32[4]{0:T(128)} %idx_hbm.3, bf16[64,512]{1,0:T(8,128)(2,1)} %rows_hbm.1), custom_call_target="tpu_custom_call" | custom-call | tf_op jit(solution)/shard_map/gather/pallas_call | solution.py:211
  2.2 6.4 %all-to-all-start = ((bf16[8,4,512]{2,1,0:T(4,128)(2,1)}), bf16[8,4,512]{2,1,0:T(4,128)(2,1)S(1)}, u32[]{:S(2)}, u32[]{:S(2)}) async-start(bf16[8,4,512]{2,1,0:T(4,128)(2,1)} %gather.1), calls=%async_computation | async-start | bytes 65536 | tf_op jit(solution)/shard_map/all_to_all | solution.py:224
  8.6 2.3 %stage.1 = (bf16[2048,512]{1,0:T(8,128)(2,1)S(1)}, f32[1,2048]{1,0:T(1,128)S(1)}, bf16[2048,256]{1,0:T(8,128)(2,1)S(1)}, f32[1,1152]{1,0:T(1,128)S(1)}) custom-call(s32[1]{0:T(128)} %bitcast.3.pos_ref, s32[1,256]{1,0:T(1,128)} %bitcast.23, f32[256,128]{1,0:T(8,128)} %eig_hbm.1, s32[4]{0:T(128)} %idx_hbm.3, f32[64,1000]{1,0:T(8,128)} %targets_hbm.1, ...), custom_call_target="tpu_custom_call" | custom-call | flops 2147483648 | bytes 16777216 | tf_op jit(solution)/shard_map/stage/pallas_call | solution.py:228
  10.9 3.4 %all-to-all-done = bf16[8,4,512]{2,1,0:T(4,128)(2,1)S(1)} async-done(((bf16[8,4,512]{2,1,0:T(4,128)(2,1)}), bf16[8,4,512]{2,1,0:T(4,128)(2,1)S(1)}, u32[]{:S(2)}, u32[]{:S(2)}) %all-to-all-start) | async-done | bytes 32800 | tf_op jit(solution)/shard_map/all_to_all | solution.py:224
  14.4 0.0 copy-start
  14.4 3.2 %share.1 = (bf16[32,2048]{1,0:T(8,128)(2,1)S(1)}, f32[288,128]{1,0:T(8,128)S(1)}, bf16[1000,2048]{1,0:T(8,128)(2,1)S(1)}) custom-call(s32[1]{0:T(128)} %bitcast.pos_ref, bf16[32,512]{1,0:T(8,128)(2,1)S(1)} %bitcast.18, bf16[2048,512]{1,0:T(8,128)(2,1)S(1)} %get-tuple-element.11.cents_ref, f32[1,2048]{1,0:T(1,128)S(1)} %get-tuple-element.12.cent_sq_ref, ...), custom_call_target="tpu_custom_call" | custom-call | tf_op jit(solution)/shard_map/share/pallas_call | solution.py:258
  17.6 11.1 %all_to_all.15 = f32[32,1,1152]{2,1,0:T(1,128)S(1)} all-to-all(f32[32,1,1152]{2,1,0:T(1,128)S(1)} %bitcast.17), channel_id=1, replica_groups=mesh['sec'=4,'wide'=8] {'sec','wide'}, dimensions={0} | all-to-all | bytes 294912 | tf_op jit(solution)/shard_map/all_to_all | solution.py:272
  28.7 10.2 %all_to_all.16 = f32[32,1,1152]{2,1,0:T(1,128)S(1)} all-to-all(f32[32,1,1152]{2,1,0:T(1,128)S(1)} %bitcast.16), channel_id=1, replica_groups=mesh['sec'=4,'wide'=8] {'sec','wide'}, dimensions={0} | all-to-all | bytes 294912 | tf_op jit(solution)/shard_map/all_to_all | solution.py:281
  38.9 0.0 copy-done
  38.9 2.6 %update.1 = (bf16[1000,2048]{1,0:T(8,128)(2,1)}, f32[4,1000]{1,0:T(4,128)}) custom-call(s32[1]{0:T(128)} %bitcast.pos_ref, f32[288,128]{1,0:T(8,128)S(1)} %bitcast.14, f32[1,128]{1,0:T(1,128)S(1)} %bitcast.19, bf16[32,2048]{1,0:T(8,128)(2,1)S(1)} %get-tuple-element.16.kern_ref, bf16[2048,256]{1,0:T(8,128)(2,1)S(1)} %get-tuple-element.13.vecs_ref, ...), custom_call_target="tpu_custom_call" | custom-call | tf_op jit(solution)/shard_map/update/pallas_call | solution.py:284
  (2 shorter events, 0.0 us)
Async XLA Ops:
  2.2 12.1 %all-to-all-start = ((bf16[8,4,512]{2,1,0:T(4,128)(2,1)}), bf16[8,4,512]{2,1,0:T(4,128)(2,1)S(1)}, u32[]{:S(2)}, u32[]{:S(2)}) async-start(bf16[8,4,512]{2,1,0:T(4,128)(2,1)} %gather.1), calls=%async_computation | async-start | bytes 65536 | tf_op jit(solution)/shard_map/all_to_all | solution.py:224
  14.4 24.5 %copy-start = (f32[128]{0:T(128)S(1)}, f32[128]{0:T(128)}, u32[]{:S(2)}) copy-start(f32[128]{0:T(128)} %param.15) | copy-start | bytes 1540

commit v6 on v5

--- a/solution.py
+++ b/solution.py
@@ -114,12 +114,16 @@
             kern_ref[:, cols] = jnp.exp((1.4142 - jnp.sqrt(dist_sq)) / length).astype(jnp.bfloat16)
         coords = dot32(kern_ref[...], vecs_ref[...], NN)
         coords = coords[:, :eig_count] + coords[:, eig_count:]
-        total = None
+        splits = list(range(0, classes, 256))
+        totals = [None] * len(splits)
         for i, get in enumerate(gets):
-            cols = pl.ds(i * step, step)
             get.wait()
-            term = dot32(kern_ref[:, cols], wt_ref[:, cols], NT)
-            total = term if total is None else total + term
+            for k in range(i * step, (i + 1) * step, 512):
+                cols = pl.ds(k, 512)
+                for n, row in enumerate(splits):
+                    term = dot32(kern_ref[:, cols], wt_ref[pl.ds(row, min(256, classes - row)), cols], NT)
+                    totals[n] = term if totals[n] is None else totals[n] + term
+        total = jnp.concatenate(totals, axis=1)
         pad = jnp.zeros((batch_total, tiles * LANES - eig_count - classes), jnp.float32)
         part = jnp.concatenate([coords, total, pad], axis=1)
         for tile in range(tiles):
@@ -165,23 +169,19 @@
     puts = []
     for start in range(0, wt_ref.shape[1], step):
         cols = pl.ds(start, step)
-        factors = factors_ref[:, cols]
         for row in range(0, classes, chunk):
-            part = pl.ds(row, min(chunk, classes - row))
-            grad = dot32(left_ref[part, :], factors, NN)
+            spot = (pl.ds(row, min(chunk, classes - row)), cols)
+            grad = dot32(left_ref[spot[0], :], factors_ref[:, cols], NN)
             grad = grad if fold else rate * grad
-            new_ref[part, cols] = (wt_ref[part, cols].astype(jnp.float32) - grad).astype(jnp.bfloat16)
-            if row // chunk % 2 == 1 or row + chunk >= classes:
-                rows = pl.ds(row // chunk // 2 * 2 * chunk, row % (2 * chunk) + part.size)
-                spot = (rows, cols)
-                puts.append(pltpu.make_async_copy(new_ref.at[spot], out_hbm.at[spot], sems.at[len(puts)]))
-                puts[-1].start()
+            new_ref[spot] = (wt_ref[spot].astype(jnp.float32) - grad).astype(jnp.bfloat16)
+            puts.append(pltpu.make_async_copy(new_ref.at[spot], out_hbm.at[spot], sems.at[len(puts)]))
+            puts[-1].start()
         if start == 0:
             for s in range(sections):
                 for tile in range(first, tiles):
                     width = min(LANES, classes - (tile - first) * LANES)
-                    row = lanes(both_ref, s * wide_count + pos_ref[0], 1, tile, tiles)[...]
-                    res_ref[pl.ds(s, 1), pl.ds((tile - first) * LANES, width)] = row[:, :width]
+                    line = lanes(both_ref, s * wide_count + pos_ref[0], 1, tile, tiles)[...]
+                    res_ref[pl.ds(s, 1), pl.ds((tile - first) * LANES, width)] = line[:, :width]
             puts.append(pltpu.make_async_copy(res_ref, res_hbm, sems.at[len(puts)]))
             puts[-1].start()
     for put in puts:
@@ -206,7 +206,7 @@
 
     params = pltpu.CompilerParams(vmem_limit_bytes=VMEM_GRANT)
     step = min(512, center_rows // 4)
-    chunk = LANES
+    chunk = 512
 
     copies = pl.pallas_call(
         gather_body,
@@ -294,7 +294,7 @@
             pltpu.VMEM((4 * batch_total, center_rows), jnp.bfloat16),
             pltpu.VMEM((classes, center_rows), jnp.bfloat16),
             pltpu.VMEM((batch_rows, classes), jnp.float32),
-            pltpu.SemaphoreType.DMA((1 + slab_count * pl.cdiv(classes, 2 * chunk),)),
+            pltpu.SemaphoreType.DMA((1 + slab_count * pl.cdiv(classes, chunk),)),
         ],
         compiler_params=params,
         name="update",

time: 41.8 us -> 41.6 us (level)
  no operation moved by 1% of the time
where the time goes in v6:
time: 41.6 us; the launch traced here: 41.3 us
  blocking collectives  21.2 us (51%)
  Pallas kernels  9.59 us (23%)
  starting transfers between devices  6.37 us (15%)
  waiting for transfers between devices  3.44 us (8%)
  between operations  0.67 us (2%)
    all_to_all x1, blocking collectives, shards(): lax.all_to_all(part.reshape(batch_total, 1, tiles * LANES), ('sec', 'wide...  11.1 us
    all_to_all x1, blocking collectives, shards(): lax.all_to_all(both.reshape(batch_total, 1, tiles * LANES), ('sec', 'wide...  10.2 us
    all_to_all x1, starting transfers between devices, shards(): piece = lax.all_to_all(copies, 'wide', 0, 0, tiled=False)  6.37 us
    all_to_all x1, waiting for transfers between devices, shards(): piece = lax.all_to_all(copies, 'wide', 0, 0, tiled=False)  3.44 us
    pallas_call x1, Pallas kernels, shards(): pl.pallas_call(functools.partial(share_body, step=step), out_shape=(jax.S...  3.03 us
    pallas_call x1, Pallas kernels, shards(): pl.pallas_call(functools.partial(update_body, rate=16.0 / batch_total, se...  2.64 us
    pallas_call x1, Pallas kernels, shards(): pl.pallas_call(functools.partial(stage_body, wide_count=wide_count), out_...  2.29 us
    pallas_call x1, Pallas kernels, shards(): pl.pallas_call(gather_body, out_shape=jax.ShapeDtypeStruct((wide_count, b...  1.6 us
  transfers between devices with their start and end apart: 1, of which 1 were waited for; matrix products, arithmetic and copies ran while one was open for 0% of the time, Pallas kernels for 6%

profile of v6, /device:TPU:0, one launch (start us, length us, event | category | flops | bytes accessed | tf_op | source)
XLA Modules:
  0.0 41.3 jit_solution(5301923122511925167)
XLA Ops:
  0.6 1.6 %gather.1 = bf16[8,4,512]{2,1,0:T(4,128)(2,1)} custom-call(s32[1]{0:T(128)} %bitcast.pos_ref, s32[4]{0:T(128)} %idx_hbm.3, bf16[64,512]{1,0:T(8,128)(2,1)} %rows_hbm.1), custom_call_target="tpu_custom_call" | custom-call | tf_op jit(solution)/shard_map/gather/pallas_call | solution.py:211
  2.2 6.4 %all-to-all-start = ((bf16[8,4,512]{2,1,0:T(4,128)(2,1)}), bf16[8,4,512]{2,1,0:T(4,128)(2,1)S(1)}, u32[]{:S(2)}, u32[]{:S(2)}) async-start(bf16[8,4,512]{2,1,0:T(4,128)(2,1)} %gather.1), calls=%async_computation | async-start | bytes 65536 | tf_op jit(solution)/shard_map/all_to_all | solution.py:224
  8.6 2.3 %stage.1 = (bf16[2048,512]{1,0:T(8,128)(2,1)S(1)}, f32[1,2048]{1,0:T(1,128)S(1)}, bf16[2048,256]{1,0:T(8,128)(2,1)S(1)}, f32[1,1152]{1,0:T(1,128)S(1)}) custom-call(s32[1]{0:T(128)} %bitcast.3.pos_ref, s32[1,256]{1,0:T(1,128)} %bitcast.23, f32[256,128]{1,0:T(8,128)} %eig_hbm.1, s32[4]{0:T(128)} %idx_hbm.3, f32[64,1000]{1,0:T(8,128)} %targets_hbm.1, ...), custom_call_target="tpu_custom_call" | custom-call | flops 2147483648 | bytes 16777216 | tf_op jit(solution)/shard_map/stage/pallas_call | solution.py:228
  10.9 3.4 %all-to-all-done = bf16[8,4,512]{2,1,0:T(4,128)(2,1)S(1)} async-done(((bf16[8,4,512]{2,1,0:T(4,128)(2,1)}), bf16[8,4,512]{2,1,0:T(4,128)(2,1)S(1)}, u32[]{:S(2)}, u32[]{:S(2)}) %all-to-all-start) | async-done | bytes 32800 | tf_op jit(solution)/shard_map/all_to_all | solution.py:224
  14.4 0.0 copy-start
  14.4 3.0 %share.1 = (bf16[32,2048]{1,0:T(8,128)(2,1)S(1)}, f32[288,128]{1,0:T(8,128)S(1)}, bf16[1000,2048]{1,0:T(8,128)(2,1)S(1)}) custom-call(s32[1]{0:T(128)} %bitcast.pos_ref, bf16[32,512]{1,0:T(8,128)(2,1)S(1)} %bitcast.18, bf16[2048,512]{1,0:T(8,128)(2,1)S(1)} %get-tuple-element.11.cents_ref, f32[1,2048]{1,0:T(1,128)S(1)} %get-tuple-element.12.cent_sq_ref, ...), custom_call_target="tpu_custom_call" | custom-call | tf_op jit(solution)/shard_map/share/pallas_call | solution.py:258
  17.4 11.1 %all_to_all.15 = f32[32,1,1152]{2,1,0:T(1,128)S(1)} all-to-all(f32[32,1,1152]{2,1,0:T(1,128)S(1)} %bitcast.17), channel_id=1, replica_groups=mesh['sec'=4,'wide'=8] {'sec','wide'}, dimensions={0} | all-to-all | bytes 294912 | tf_op jit(solution)/shard_map/all_to_all | solution.py:272
  28.5 10.2 %all_to_all.16 = f32[32,1,1152]{2,1,0:T(1,128)S(1)} all-to-all(f32[32,1,1152]{2,1,0:T(1,128)S(1)} %bitcast.16), channel_id=1, replica_groups=mesh['sec'=4,'wide'=8] {'sec','wide'}, dimensions={0} | all-to-all | bytes 294912 | tf_op jit(solution)/shard_map/all_to_all | solution.py:281
  38.7 0.0 copy-done
  38.7 2.6 %update.1 = (bf16[1000,2048]{1,0:T(8,128)(2,1)}, f32[4,1000]{1,0:T(4,128)}) custom-call(s32[1]{0:T(128)} %bitcast.pos_ref, f32[288,128]{1,0:T(8,128)S(1)} %bitcast.14, f32[1,128]{1,0:T(1,128)S(1)} %bitcast.19, bf16[32,2048]{1,0:T(8,128)(2,1)S(1)} %get-tuple-element.16.kern_ref, bf16[2048,256]{1,0:T(8,128)(2,1)S(1)} %get-tuple-element.13.vecs_ref, ...), custom_call_target="tpu_custom_call" | custom-call | tf_op jit(solution)/shard_map/update/pallas_call | solution.py:284
  (2 shorter events, 0.0 us)
Async XLA Ops:
  2.2 12.1 %all-to-all-start = ((bf16[8,4,512]{2,1,0:T(4,128)(2,1)}), bf16[8,4,512]{2,1,0:T(4,128)(2,1)S(1)}, u32[]{:S(2)}, u32[]{:S(2)}) async-start(bf16[8,4,512]{2,1,0:T(4,128)(2,1)} %gather.1), calls=%async_computation | async-start | bytes 65536 | tf_op jit(solution)/shard_map/all_to_all | solution.py:224
  14.4 24.3 %copy-start = (f32[128]{0:T(128)S(1)}, f32[128]{0:T(128)}, u32[]{:S(2)}) copy-start(f32[128]{0:T(128)} %param.15) | copy-start | bytes 1540

commit v7 on v6

--- a/solution.py
+++ b/solution.py
@@ -9,6 +9,7 @@
 from jax.sharding import PartitionSpec as P
 
 LANES = 128
+LINES = 4
 VMEM_GRANT = 16 << 20
 NT = (((1,), (1,)), ((), ()))
 NN = (((1,), (0,)), ((), ()))
@@ -131,33 +132,55 @@
                 lanes(part_ref, row, 8, tile, tiles)[...] = part[row : row + 8, tile * LANES : (tile + 1) * LANES]
 
 
-def settle_body(parts_ref, wanted_ref, both_ref, *, count):
+def settle_body(parts_ref, wanted_ref, both_ref, *, first):
+    count, lines, width = both_ref.shape
     tiles = parts_ref.shape[0] // count
+    pieces = []
+    coords = []
     for tile in range(tiles):
         total = jnp.sum(lanes(parts_ref, 0, count, tile, tiles)[...], axis=0, keepdims=True)
         total = total - wanted_ref[:, tile * LANES : (tile + 1) * LANES]
-        lanes(both_ref, 0, count, tile, tiles)[...] = jnp.broadcast_to(total, (count, LANES))
+        (coords if tile < first else pieces).append(total)
+    for _ in range(3):
+        pieces += [total.astype(jnp.bfloat16).astype(jnp.float32) for total in coords]
+        coords = [total - piece for total, piece in zip(coords, pieces[-first:])]
+    blocks = width // LANES
+    pieces += [jnp.zeros_like(pieces[0])] * (lines * blocks - len(pieces))
+    out = jnp.zeros((lines, width), jnp.float32)
+    for line in range(lines):
+        whole = jnp.concatenate(pieces[line * blocks : (line + 1) * blocks], axis=1)
+        out = jnp.where(lax.broadcasted_iota(jnp.int32, out.shape, 0) == line, whole, out)
+    out = out.astype(jnp.bfloat16)
+    for device in range(count):
+        both_ref[device] = out
 
 
 def update_body(
     pos_ref, both_ref, scale_ref, kern_ref, vecs_ref, wt_ref, out_hbm, res_hbm,
-    left_ref, factors_ref, new_ref, res_ref, sems, *, rate, sections, step, chunk
+    flat_ref, left_ref, factors_ref, new_ref, res_ref, sems, *, rate, sections, step, chunk
 ):
     fold = math.frexp(rate)[0] == 0.5
     classes = wt_ref.shape[0]
-    batch_total = kern_ref.shape[0]
+    batch_total, lines, width = both_ref.shape
+    wide_count = batch_total // sections
+    blocks = width // LANES
     eig_count = vecs_ref.shape[1] // 2
     first = eig_count // LANES
-    tiles = both_ref.shape[0] // batch_total
-    wide_count = batch_total // sections
-    for tile in range(first, tiles):
-        rows = lanes(both_ref, 0, batch_total, tile, tiles)[...].astype(jnp.bfloat16)
-        if fold:
-            rows = (rows.astype(jnp.float32) * rate).astype(jnp.bfloat16)
-        turned = jnp.concatenate([rows, rows, rows, rows], axis=0).T
-        left_ref[pl.ds((tile - first) * LANES, LANES), :] = turned
-    coords = jnp.concatenate([lanes(both_ref, 0, batch_total, tile, tiles)[...] for tile in range(first)], axis=1)
-    coords_hi, coords_lo = halves(coords * scale_ref[...])
+    res_tiles = pl.cdiv(classes, LANES)
+    flat = both_ref[...].astype(jnp.float32).reshape(batch_total * lines, width)
+    for block in range(blocks):
+        flat_ref[pl.ds(block * batch_total * lines, batch_total * lines), :] = flat[:, block * LANES : (block + 1) * LANES]
+
+    def piece(tile, row, count):
+        line, block = divmod(tile, blocks)
+        return flat_ref[pl.ds((block * batch_total + row) * lines + line, count, stride=lines), :]
+
+    for tile in range(res_tiles):
+        rows = piece(tile, 0, batch_total)
+        rows = (rows * rate if fold else rows).astype(jnp.bfloat16)
+        left_ref[pl.ds(tile * LANES, LANES), :] = jnp.concatenate([rows, rows, rows, rows], axis=0).T
+    parts = [jnp.concatenate([piece(res_tiles + i * first + tile, 0, batch_total) for tile in range(first)], axis=1) for i in range(3)]
+    coords_hi, coords_lo = halves((parts[0] + parts[1] + parts[2]) * scale_ref[...])
     coords = jnp.concatenate([coords_hi, coords_lo], axis=0)
     coords = jnp.concatenate([coords, coords], axis=1)
     for start in range(0, wt_ref.shape[1], step):
@@ -178,10 +201,10 @@
             puts[-1].start()
         if start == 0:
             for s in range(sections):
-                for tile in range(first, tiles):
-                    width = min(LANES, classes - (tile - first) * LANES)
-                    line = lanes(both_ref, s * wide_count + pos_ref[0], 1, tile, tiles)[...]
-                    res_ref[pl.ds(s, 1), pl.ds((tile - first) * LANES, width)] = line[:, :width]
+                for tile in range(res_tiles):
+                    size = min(LANES, classes - tile * LANES)
+                    line = piece(tile, s * wide_count + pos_ref[0], 1)
+                    res_ref[pl.ds(s, 1), pl.ds(tile * LANES, size)] = line[:, :size]
             puts.append(pltpu.make_async_copy(res_ref, res_hbm, sems.at[len(puts)]))
             puts[-1].start()
     for put in puts:
@@ -270,16 +293,17 @@
     )(wide_pos[None], piece, staged_centers, cent_sq, vecs, turned_weights)
 
     parts = lax.all_to_all(part.reshape(batch_total, 1, tiles * LANES), ("sec", "wide"), 0, 0, tiled=False)
+    first = eig_count // LANES
+    blocks = pl.cdiv(tiles + 2 * first, LINES)
     both = pl.pallas_call(
-        functools.partial(settle_body, count=batch_total),
-        out_shape=jax.ShapeDtypeStruct((batch_total * tiles, LANES), jnp.float32),
+        functools.partial(settle_body, first=first),
+        out_shape=jax.ShapeDtypeStruct((batch_total, LINES, blocks * LANES), jnp.bfloat16),
         in_specs=[vmem, vmem],
         out_specs=vmem,
         compiler_params=params,
         name="settle",
     )(parts.reshape(batch_total * tiles, LANES), wanted)
-    both = lax.all_to_all(both.reshape(batch_total, 1, tiles * LANES), ("sec", "wide"), 0, 0, tiled=False)
-    both = both.reshape(batch_total * tiles, LANES)
+    both = lax.all_to_all(both, ("sec", "wide"), 0, 0, tiled=False)
 
     new_turned, residual = pl.pallas_call(
         functools.partial(update_body, rate=16.0 / batch_total, sections=sec_count, step=step, chunk=chunk),
@@ -290,6 +314,7 @@
         in_specs=[smem] + [vmem] * 5,
         out_specs=(hbm, hbm),
         scratch_shapes=[
+            pltpu.VMEM((blocks * batch_total * LINES, LANES), jnp.float32),
             pltpu.VMEM((pl.cdiv(classes, LANES) * LANES, 4 * batch_total), jnp.bfloat16),
             pltpu.VMEM((4 * batch_total, center_rows), jnp.bfloat16),
             pltpu.VMEM((classes, center_rows), jnp.bfloat16),

time: 41.6 us -> 41 us (0.986)
  blocking collectives: 21.2 us -> 20.6 us
    all_to_all x1, blocking collectives: 10.2 us -> 9.56 us  [shards(): both = lax.all_to_all(both, ('sec', 'wide'), 0, 0, tiled=False)]
where the time goes in v7:
time: 41 us; the launch traced here: 40.7 us
  blocking collectives  20.6 us (50%)
  Pallas kernels  9.61 us (23%)
  starting transfers between devices  6.37 us (16%)
  waiting for transfers between devices  3.43 us (8%)
  between operations  0.67 us (2%)
    all_to_all x1, blocking collectives, shards(): lax.all_to_all(part.reshape(batch_total, 1, tiles * LANES), ('sec', 'wide...  11.1 us
    all_to_all x1, blocking collectives, shards(): both = lax.all_to_all(both, ('sec', 'wide'), 0, 0, tiled=False)  9.56 us
    all_to_all x1, starting transfers between devices, shards(): piece = lax.all_to_all(copies, 'wide', 0, 0, tiled=False)  6.37 us
    all_to_all x1, waiting for transfers between devices, shards(): piece = lax.all_to_all(copies, 'wide', 0, 0, tiled=False)  3.43 us
    pallas_call x1, Pallas kernels, shards(): pl.pallas_call(functools.partial(share_body, step=step), out_shape=(jax.S...  3.03 us
    pallas_call x1, Pallas kernels, shards(): pl.pallas_call(functools.partial(update_body, rate=16.0 / batch_total, se...  2.66 us
    pallas_call x1, Pallas kernels, shards(): pl.pallas_call(functools.partial(stage_body, wide_count=wide_count), out_...  2.29 us
    pallas_call x1, Pallas kernels, shards(): pl.pallas_call(gather_body, out_shape=jax.ShapeDtypeStruct((wide_count, b...  1.6 us
  transfers between devices with their start and end apart: 1, of which 1 were waited for; matrix products, arithmetic and copies ran while one was open for 0% of the time, Pallas kernels for 6%

profile of v7, /device:TPU:0, one launch (start us, length us, event | category | flops | bytes accessed | tf_op | source)
XLA Modules:
  0.0 40.7 jit_solution(16647660912938713773)
XLA Ops:
  0.6 1.6 %gather.1 = bf16[8,4,512]{2,1,0:T(4,128)(2,1)} custom-call(s32[1]{0:T(128)} %bitcast.pos_ref, s32[4]{0:T(128)} %idx_hbm.3, bf16[64,512]{1,0:T(8,128)(2,1)} %rows_hbm.1), custom_call_target="tpu_custom_call" | custom-call | tf_op jit(solution)/shard_map/gather/pallas_call | solution.py:234
  2.2 6.4 %all-to-all-start = ((bf16[8,4,512]{2,1,0:T(4,128)(2,1)}), bf16[8,4,512]{2,1,0:T(4,128)(2,1)S(1)}, u32[]{:S(2)}, u32[]{:S(2)}) async-start(bf16[8,4,512]{2,1,0:T(4,128)(2,1)} %gather.1), calls=%async_computation | async-start | bytes 65536 | tf_op jit(solution)/shard_map/all_to_all | solution.py:247
  8.6 2.3 %stage.1 = (bf16[2048,512]{1,0:T(8,128)(2,1)S(1)}, f32[1,2048]{1,0:T(1,128)S(1)}, bf16[2048,256]{1,0:T(8,128)(2,1)S(1)}, f32[1,1152]{1,0:T(1,128)S(1)}) custom-call(s32[1]{0:T(128)} %bitcast.3.pos_ref, s32[1,256]{1,0:T(1,128)} %bitcast.19, f32[256,128]{1,0:T(8,128)} %eig_hbm.1, s32[4]{0:T(128)} %idx_hbm.3, f32[64,1000]{1,0:T(8,128)} %targets_hbm.1, ...), custom_call_target="tpu_custom_call" | custom-call | flops 2147483648 | bytes 16777216 | tf_op jit(solution)/shard_map/stage/pallas_call | solution.py:251
  10.9 0.0 copy-start
  10.9 3.4 %all-to-all-done = bf16[8,4,512]{2,1,0:T(4,128)(2,1)S(1)} async-done(((bf16[8,4,512]{2,1,0:T(4,128)(2,1)}), bf16[8,4,512]{2,1,0:T(4,128)(2,1)S(1)}, u32[]{:S(2)}, u32[]{:S(2)}) %all-to-all-start) | async-done | bytes 32800 | tf_op jit(solution)/shard_map/all_to_all | solution.py:247
  14.4 3.0 %share.1 = (bf16[32,2048]{1,0:T(8,128)(2,1)S(1)}, f32[288,128]{1,0:T(8,128)S(1)}, bf16[1000,2048]{1,0:T(8,128)(2,1)S(1)}) custom-call(s32[1]{0:T(128)} %bitcast.pos_ref, bf16[32,512]{1,0:T(8,128)(2,1)S(1)} %bitcast.14, bf16[2048,512]{1,0:T(8,128)(2,1)S(1)} %get-tuple-element.11.cents_ref, f32[1,2048]{1,0:T(1,128)S(1)} %get-tuple-element.12.cent_sq_ref, ...), custom_call_target="tpu_custom_call" | custom-call | tf_op jit(solution)/shard_map/share/pallas_call | solution.py:281
  17.4 11.1 %all_to_all.15 = f32[32,1,1152]{2,1,0:T(1,128)S(1)} all-to-all(f32[32,1,1152]{2,1,0:T(1,128)S(1)} %bitcast.13), channel_id=1, replica_groups=mesh['sec'=4,'wide'=8] {'sec','wide'}, dimensions={0} | all-to-all | bytes 294912 | tf_op jit(solution)/shard_map/all_to_all | solution.py:295
  28.5 9.6 %all_to_all.16.both_ref = bf16[32,4,384]{2,1,0:T(4,128)(2,1)S(1)} all-to-all(bf16[32,4,384]{2,1,0:T(4,128)(2,1)S(1)} %settle.1), channel_id=1, replica_groups=mesh['sec'=4,'wide'=8] {'sec','wide'}, dimensions={0} | all-to-all | bytes 196608 | tf_op jit(solution)/shard_map/all_to_all | solution.py:306
  38.1 0.0 copy-done
  38.1 2.7 %update.1 = (bf16[1000,2048]{1,0:T(8,128)(2,1)}, f32[4,1000]{1,0:T(4,128)}) custom-call(s32[1]{0:T(128)} %bitcast.pos_ref, bf16[32,4,384]{2,1,0:T(4,128)(2,1)S(1)} %all_to_all.16.both_ref, f32[1,128]{1,0:T(1,128)S(1)} %bitcast.15, bf16[32,2048]{1,0:T(8,128)(2,1)S(1)} %get-tuple-element.16.kern_ref, bf16[2048,256]{1,0:T(8,128)(2,1)S(1)} %get-tuple-element.13.vecs_ref, ...), custom_call_target="tpu_custom_call" | custom-call | tf_op jit(solution)/shard_map/update/pallas_call | solution.py:308
  (2 shorter events, 0.0 us)
Async XLA Ops:
  2.2 12.1 %all-to-all-start = ((bf16[8,4,512]{2,1,0:T(4,128)(2,1)}), bf16[8,4,512]{2,1,0:T(4,128)(2,1)S(1)}, u32[]{:S(2)}, u32[]{:S(2)}) async-start(bf16[8,4,512]{2,1,0:T(4,128)(2,1)} %gather.1), calls=%async_computation | async-start | bytes 65536 | tf_op jit(solution)/shard_map/all_to_all | solution.py:247
  10.9 27.2 %copy-start = (f32[128]{0:T(128)S(1)}, f32[128]{0:T(128)}, u32[]{:S(2)}) copy-start(f32[128]{0:T(128)} %param.15) | copy-start | bytes 1540

commit v8 on v7

--- a/solution.py
+++ b/solution.py
@@ -183,15 +183,19 @@
     coords_hi, coords_lo = halves((parts[0] + parts[1] + parts[2]) * scale_ref[...])
     coords = jnp.concatenate([coords_hi, coords_lo], axis=0)
     coords = jnp.concatenate([coords, coords], axis=1)
-    for start in range(0, wt_ref.shape[1], step):
+    def make(start):
         cols = pl.ds(start, step)
         drop = dot32(coords, vecs_ref[cols, :], NT)
         drop = drop[:batch_total] + drop[batch_total:]
         drop_hi, drop_lo = halves(-drop)
         factors_ref[:, cols] = jnp.concatenate([kern_ref[:, cols], drop_hi, drop_lo, jnp.zeros_like(drop_lo)], axis=0)
+
+    make(0)
     puts = []
     for start in range(0, wt_ref.shape[1], step):
         cols = pl.ds(start, step)
+        if start + step < wt_ref.shape[1]:
+            make(start + step)
         for row in range(0, classes, chunk):
             spot = (pl.ds(row, min(chunk, classes - row)), cols)
             grad = dot32(left_ref[spot[0], :], factors_ref[:, cols], NN)

time: 41 us -> 40.9 us (level)
  no operation moved by 1% of the time
where the time goes in v8:
time: 40.9 us; the launch traced here: 40.6 us
  blocking collectives  20.6 us (50%)
  Pallas kernels  9.5 us (23%)
  starting transfers between devices  6.37 us (16%)
  waiting for transfers between devices  3.43 us (8%)
  between operations  0.67 us (2%)
    all_to_all x1, blocking collectives, shards(): lax.all_to_all(part.reshape(batch_total, 1, tiles * LANES), ('sec', 'wide...  11.1 us
    all_to_all x1, blocking collectives, shards(): both = lax.all_to_all(both, ('sec', 'wide'), 0, 0, tiled=False)  9.56 us
    all_to_all x1, starting transfers between devices, shards(): piece = lax.all_to_all(copies, 'wide', 0, 0, tiled=False)  6.37 us
    all_to_all x1, waiting for transfers between devices, shards(): piece = lax.all_to_all(copies, 'wide', 0, 0, tiled=False)  3.43 us
    pallas_call x1, Pallas kernels, shards(): pl.pallas_call(functools.partial(share_body, step=step), out_shape=(jax.S...  3.03 us
    pallas_call x1, Pallas kernels, shards(): pl.pallas_call(functools.partial(update_body, rate=16.0 / batch_total, se...  2.55 us
    pallas_call x1, Pallas kernels, shards(): pl.pallas_call(functools.partial(stage_body, wide_count=wide_count), out_...  2.29 us
    pallas_call x1, Pallas kernels, shards(): pl.pallas_call(gather_body, out_shape=jax.ShapeDtypeStruct((wide_count, b...  1.6 us
  transfers between devices with their start and end apart: 1, of which 1 were waited for; matrix products, arithmetic and copies ran while one was open for 0% of the time, Pallas kernels for 6%

profile of v8, /device:TPU:0, one launch (start us, length us, event | category | flops | bytes accessed | tf_op | source)
XLA Modules:
  0.0 40.6 jit_solution(2190298556640791766)
XLA Ops:
  0.6 1.6 %gather.1 = bf16[8,4,512]{2,1,0:T(4,128)(2,1)} custom-call(s32[1]{0:T(128)} %bitcast.pos_ref, s32[4]{0:T(128)} %idx_hbm.3, bf16[64,512]{1,0:T(8,128)(2,1)} %rows_hbm.1), custom_call_target="tpu_custom_call" | custom-call | tf_op jit(solution)/shard_map/gather/pallas_call | solution.py:238
  2.2 6.4 %all-to-all-start = ((bf16[8,4,512]{2,1,0:T(4,128)(2,1)}), bf16[8,4,512]{2,1,0:T(4,128)(2,1)S(1)}, u32[]{:S(2)}, u32[]{:S(2)}) async-start(bf16[8,4,512]{2,1,0:T(4,128)(2,1)} %gather.1), calls=%async_computation | async-start | bytes 65536 | tf_op jit(solution)/shard_map/all_to_all | solution.py:251
  8.6 2.3 %stage.1 = (bf16[2048,512]{1,0:T(8,128)(2,1)S(1)}, f32[1,2048]{1,0:T(1,128)S(1)}, bf16[2048,256]{1,0:T(8,128)(2,1)S(1)}, f32[1,1152]{1,0:T(1,128)S(1)}) custom-call(s32[1]{0:T(128)} %bitcast.3.pos_ref, s32[1,256]{1,0:T(1,128)} %bitcast.19, f32[256,128]{1,0:T(8,128)} %eig_hbm.1, s32[4]{0:T(128)} %idx_hbm.3, f32[64,1000]{1,0:T(8,128)} %targets_hbm.1, ...), custom_call_target="tpu_custom_call" | custom-call | flops 2147483648 | bytes 16777216 | tf_op jit(solution)/shard_map/stage/pallas_call | solution.py:255
  10.9 0.0 copy-start
  10.9 3.4 %all-to-all-done = bf16[8,4,512]{2,1,0:T(4,128)(2,1)S(1)} async-done(((bf16[8,4,512]{2,1,0:T(4,128)(2,1)}), bf16[8,4,512]{2,1,0:T(4,128)(2,1)S(1)}, u32[]{:S(2)}, u32[]{:S(2)}) %all-to-all-start) | async-done | bytes 32800 | tf_op jit(solution)/shard_map/all_to_all | solution.py:251
  14.4 3.0 %share.1 = (bf16[32,2048]{1,0:T(8,128)(2,1)S(1)}, f32[288,128]{1,0:T(8,128)S(1)}, bf16[1000,2048]{1,0:T(8,128)(2,1)S(1)}) custom-call(s32[1]{0:T(128)} %bitcast.pos_ref, bf16[32,512]{1,0:T(8,128)(2,1)S(1)} %bitcast.14, bf16[2048,512]{1,0:T(8,128)(2,1)S(1)} %get-tuple-element.11.cents_ref, f32[1,2048]{1,0:T(1,128)S(1)} %get-tuple-element.12.cent_sq_ref, ...), custom_call_target="tpu_custom_call" | custom-call | tf_op jit(solution)/shard_map/share/pallas_call | solution.py:285
  17.4 11.1 %all_to_all.15 = f32[32,1,1152]{2,1,0:T(1,128)S(1)} all-to-all(f32[32,1,1152]{2,1,0:T(1,128)S(1)} %bitcast.13), channel_id=1, replica_groups=mesh['sec'=4,'wide'=8] {'sec','wide'}, dimensions={0} | all-to-all | bytes 294912 | tf_op jit(solution)/shard_map/all_to_all | solution.py:299
  28.5 9.6 %all_to_all.16.both_ref = bf16[32,4,384]{2,1,0:T(4,128)(2,1)S(1)} all-to-all(bf16[32,4,384]{2,1,0:T(4,128)(2,1)S(1)} %settle.1), channel_id=1, replica_groups=mesh['sec'=4,'wide'=8] {'sec','wide'}, dimensions={0} | all-to-all | bytes 196608 | tf_op jit(solution)/shard_map/all_to_all | solution.py:310
  38.1 0.0 copy-done
  38.1 2.5 %update.1 = (bf16[1000,2048]{1,0:T(8,128)(2,1)}, f32[4,1000]{1,0:T(4,128)}) custom-call(s32[1]{0:T(128)} %bitcast.pos_ref, bf16[32,4,384]{2,1,0:T(4,128)(2,1)S(1)} %all_to_all.16.both_ref, f32[1,128]{1,0:T(1,128)S(1)} %bitcast.15, bf16[32,2048]{1,0:T(8,128)(2,1)S(1)} %get-tuple-element.16.kern_ref, bf16[2048,256]{1,0:T(8,128)(2,1)S(1)} %get-tuple-element.13.vecs_ref, ...), custom_call_target="tpu_custom_call" | custom-call | tf_op jit(solution)/shard_map/update/pallas_call | solution.py:312
  (2 shorter events, 0.0 us)
Async XLA Ops:
  2.2 12.1 %all-to-all-start = ((bf16[8,4,512]{2,1,0:T(4,128)(2,1)}), bf16[8,4,512]{2,1,0:T(4,128)(2,1)S(1)}, u32[]{:S(2)}, u32[]{:S(2)}) async-start(bf16[8,4,512]{2,1,0:T(4,128)(2,1)} %gather.1), calls=%async_computation | async-start | bytes 65536 | tf_op jit(solution)/shard_map/all_to_all | solution.py:251
  10.9 27.2 %copy-start = (f32[128]{0:T(128)S(1)}, f32[128]{0:T(128)}, u32[]{:S(2)}) copy-start(f32[128]{0:T(128)} %param.15) | copy-start | bytes 1540
